TPU v7x, 512 devices: a whole 4x8x8 slice. The times are simulated.
512 devices in a mesh: ctx: 16 (over z, x_hi), head: 32 (over y, x_lo, core).
Axes of the slice: x: 4 (x_hi: 2, x_lo: 2; x = x_hi * 2 + x_lo), y: 8, z: 8, core: 2. Of those that a mesh axis runs over, the one named last changes fastest.
Arguments:
- x_in: bfloat16 [4096, 16384], P('ctx', 'head'), may hold values from -64 to 64
- z_in: bfloat16 [4096, 16384], P('ctx', 'head'), may hold values from -6 to 6
- bc_in: bfloat16 [4096, 2048], P('ctx'), may hold values from -0.8984375 to 0.8984375
- dt_raw: float32 [256, 4096], P('head', 'ctx'), may hold values from -2 to 4
- a_log: float32 [256], P('head'), may hold values from -12 to -3
- d_skip: float32 [256], P('head'), may hold values from 0.5 to 1.5
- conv_x: bfloat16 [4, 16384], P(None, 'head'), may hold values from -3 to 3
- conv_bc: bfloat16 [4, 2048], replicated, may hold values from -3 to 3
- norm_gain: float32 [16384], P('head'), may hold values from 0.5 to 1.5
- queries: bfloat16 [4096, 8192], P('ctx', 'head'), may hold values from -160 to 160
- keys_values: bfloat16 [2, 4096, 1024], P(None, 'ctx'), may hold values from -10 to 10
Outputs:
- ssm_out: bfloat16 [4096, 16384], P('ctx', 'head')
- attn_out: bfloat16 [4096, 8192], P('ctx', 'head')
All inputs are finite; a program needn't handle non-finite values.
Results may differ from a plain program's by a relative error of at most 0.008.
Values may be sent and summed in bfloat16 or wider, within the bound.
A program may use at most 64 MiB of HBM per device.

v0:
```python
import math

import jax
import jax.numpy as jnp
from jax import lax
from jax.sharding import PartitionSpec as P

SSM_HEADS = 256
SSM_HEAD_DIM = 64
STATE = 128
GROUPS = 8
Q_HEADS = 64
KV_HEADS = 8
HEAD_DIM = 128
CONV = 4
BLOCK = 128


EPSILON = 1e-05
NEGATIVE = -1e30
HIGH = lax.Precision.HIGHEST


def from_behind(x, axis, by):
    count = lax.axis_size(axis)
    pairs = [(i, i + by) for i in range(count) if 0 <= i + by < count]
    return lax.ppermute(x, axis, pairs)


def carried_in(x, axis, join, neutral):
    place = lax.axis_index(axis)
    gathered = jax.tree.map(
        lambda a, kind: lax.all_gather(a.astype(kind), axis), x, (jnp.bfloat16, jnp.bfloat16)
    )
    state = jax.tree.map(lambda a, e: jnp.zeros_like(a) + jnp.asarray(e, a.dtype), x, neutral)

    def one(lap, state):
        return join(
            state,
            jax.tree.map(
                lambda a, own: lax.dynamic_index_in_dim(a, lap, 0, False).astype(own.dtype),
                gathered,
                x,
            ),
        )

    return lax.fori_loop(0, place, one, state)


def convolve(padded, conv_taps, tok_rows):
    total_sum = jnp.zeros((tok_rows, padded.shape[1]), jnp.float32)
    for offset in range(conv_taps.shape[0]):
        total_sum = total_sum + padded[offset : offset + tok_rows].astype(jnp.float32) * conv_taps[
            offset
        ].astype(jnp.float32)
    return jax.nn.silu(total_sum).astype(jnp.bfloat16)


def combine(earlier, later):
    return (earlier[0] + later[0], jnp.exp(later[0])[:, None, None] * earlier[1] + later[1])


def local(
    x_in, z_in, bc_in, dt_raw, a_log, d_skip, conv_x, conv_bc, norm_gain, queries, keys_values
):
    tok_rows = x_in.shape[0]
    head_count = dt_raw.shape[0]
    per_group = SSM_HEADS // GROUPS
    ctx_index = lax.axis_index("ctx")
    head_index = lax.axis_index("head")
    group_index = head_index * head_count // per_group
    b_cols = lax.dynamic_slice_in_dim(bc_in, group_index * STATE, STATE, 1)
    c_cols = lax.dynamic_slice_in_dim(bc_in, GROUPS * STATE + group_index * STATE, STATE, 1)
    group_bc = jnp.concatenate([b_cols, c_cols], axis=1)
    taps_b = lax.dynamic_slice_in_dim(conv_bc, group_index * STATE, STATE, 1)
    taps_c = lax.dynamic_slice_in_dim(conv_bc, GROUPS * STATE + group_index * STATE, STATE, 1)
    group_taps = jnp.concatenate([taps_b, taps_c], axis=1)
    rim_rows = CONV - 1
    prev_x, prev_bc = from_behind(
        (x_in[tok_rows - rim_rows :], group_bc[tok_rows - rim_rows :]), "ctx", 1
    )
    x_conv = convolve(jnp.concatenate([prev_x, x_in], axis=0), conv_x, tok_rows)
    bc_conv = convolve(jnp.concatenate([prev_bc, group_bc], axis=0), group_taps, tok_rows)
    block_count = tok_rows // BLOCK
    x_blocks = x_conv.reshape(block_count, BLOCK, head_count, SSM_HEAD_DIM)
    b_blocks = bc_conv[:, :STATE].reshape(block_count, BLOCK, STATE)
    c_blocks = bc_conv[:, STATE:].reshape(block_count, BLOCK, STATE)
    step_size = jax.nn.softplus(dt_raw)
    log_rate = -jnp.exp(a_log)[:, None] * step_size
    step_blocks = step_size.reshape(head_count, block_count, BLOCK)
    cum_rate = jnp.cumsum(log_rate.reshape(head_count, block_count, BLOCK), axis=2)
    scores = jnp.einsum("ktn,ksn->kts", c_blocks, b_blocks, preferred_element_type=jnp.float32)
    lower_mask = jnp.tril(jnp.ones((BLOCK, BLOCK), dtype=bool))
    rate_gap = jnp.minimum(cum_rate[:, :, :, None] - cum_rate[:, :, None, :], 0.0)
    decays = jnp.where(lower_mask, jnp.exp(rate_gap), 0.0)
    weights = (scores[None] * decays * step_blocks[:, :, None, :]).astype(jnp.bfloat16)
    diag_term = jnp.einsum("hkts,kshp->kthp", weights, x_blocks, preferred_element_type=jnp.float32)
    tail_decay = jnp.exp(cum_rate[:, :, -1:] - cum_rate) * step_blocks
    carried = (tail_decay.transpose(1, 2, 0)[:, :, :, None] * x_blocks).astype(jnp.bfloat16)
    block_state = jnp.einsum(
        "kshp,ksn->khpn", carried, b_blocks, preferred_element_type=jnp.float32
    )
    block_last = cum_rate[:, :, -1]
    running = jnp.zeros((head_count, SSM_HEAD_DIM, STATE), jnp.float32)
    starts = []
    for block_index in range(block_count):
        starts.append(running)
        running = (
            jnp.exp(block_last[:, block_index])[:, None, None] * running + block_state[block_index]
        )
    log_total = jnp.sum(block_last, axis=1)
    identity = (jnp.zeros_like(log_total), jnp.zeros_like(running))
    _, incoming = carried_in((log_total, running), "ctx", combine, identity)
    before = jnp.cumsum(block_last, axis=1) - block_last
    entering = jnp.stack(starts) + jnp.exp(before).T[:, :, None, None] * incoming[None]
    reach_term = jnp.einsum(
        "ktn,khpn->kthp", c_blocks.astype(jnp.float32), entering, precision=HIGH
    )
    offdiag = reach_term * jnp.exp(cum_rate).transpose(1, 2, 0)[:, :, :, None]
    ssm_raw = diag_term + offdiag + d_skip[None, None, :, None] * x_blocks
    ssm_raw = ssm_raw.reshape(tok_rows, head_count * SSM_HEAD_DIM)
    gated_out = ssm_raw * jax.nn.silu(z_in.astype(jnp.float32))
    local_squares = jnp.sum(gated_out * gated_out, axis=1)
    group_stat = jnp.where(jnp.arange(GROUPS)[:, None] == group_index, local_squares[None, :], 0.0)
    summed = lax.psum(group_stat, "head")
    group_total = lax.dynamic_slice_in_dim(summed, group_index, 1, 0)[0]
    mean_square = group_total / (per_group * SSM_HEAD_DIM)
    ssm_out = (gated_out * lax.rsqrt(mean_square + EPSILON)[:, None] * norm_gain[None, :]).astype(
        jnp.bfloat16
    )
    q_count = queries.shape[1] // HEAD_DIM
    per_kv = Q_HEADS // KV_HEADS
    kv_index = head_index * q_count // per_kv
    kv_mine = lax.dynamic_slice_in_dim(keys_values, kv_index * HEAD_DIM, HEAD_DIM, 2)
    query_heads = queries.reshape(tok_rows, q_count, HEAD_DIM)
    own_rows = ctx_index * tok_rows + jnp.arange(tok_rows)
    last_row = ctx_index * tok_rows + tok_rows - 1
    score_scale = 1.0 / math.sqrt(HEAD_DIM)
    initial = (
        jnp.full((q_count, tok_rows), NEGATIVE, jnp.float32),
        jnp.zeros((q_count, tok_rows), jnp.float32),
        jnp.zeros((q_count, tok_rows, HEAD_DIM), jnp.float32),
    )
    piece = lax.all_gather(kv_mine, "ctx", axis=1, tiled=True)
    start = jnp.int32(0)

    def work(running_state):
        row_top, row_total, weighted = running_state
        for offset in range(0, piece.shape[1], 1024):
            segment = piece[:, offset : offset + 1024]
            key_rows = start + offset + jnp.arange(segment.shape[1])
            visible = own_rows[:, None] >= key_rows[None, :]
            logits = (
                jnp.einsum(
                    "thd,sd->hts", query_heads, segment[0], preferred_element_type=jnp.float32
                )
                * score_scale
            )
            logits = jnp.where(visible[None], logits, NEGATIVE)
            new_top = jnp.maximum(row_top, jnp.max(logits, axis=2))
            shrink = jnp.exp(row_top - new_top)
            exp_scores = jnp.where(visible[None], jnp.exp(logits - new_top[:, :, None]), 0.0)
            row_total = row_total * shrink + jnp.sum(exp_scores, axis=2)
            weighted = weighted * shrink[:, :, None] + jnp.einsum(
                "hts,sd->htd",
                exp_scores.astype(jnp.bfloat16),
                segment[1],
                preferred_element_type=jnp.float32,
            )
            row_top = new_top
        return (row_top, row_total, weighted)

    row_top, row_total, weighted = lax.cond(start <= last_row, work, lambda kept: kept, initial)
    attn_out = (
        (weighted / row_total[:, :, None])
        .transpose(1, 0, 2)
        .reshape(tok_rows, q_count * HEAD_DIM)
        .astype(jnp.bfloat16)
    )
    return (ssm_out, attn_out)


def solution(mesh):
    placed = (
        P("ctx", "head"),
        P("ctx", "head"),
        P("ctx", None),
        P("head", "ctx"),
        P("head"),
        P("head"),
        P(None, "head"),
        P(),
        P("head"),
        P("ctx", "head"),
        P(None, "ctx", None),
    )
    return jax.shard_map(
        local,
        mesh=mesh,
        in_specs=placed,
        out_specs=(P("ctx", "head"), P("ctx", "head")),
        check_vma=False,
    )
```

profile of v0, /device:TPU:448, one launch (start us, length us, event | category | flops | bytes accessed | tf_op | source)
XLA Modules:
  0.0 270.6 jit_solution(1856470974735523038)
XLA Ops:
  7.2 1.1 copy-done
  10.1 4.9 %collective-permute-start.1 = (bf16[3,256]{1,0:T(4,128)(2,1)S(1)}, bf16[3,256]{1,0:T(4,128)(2,1)S(1)}, u32[]{:S(2)}, u32[]{:S(2)}) collective-permute-start(bf16[3,256]{1,0:T(4,128)(2,1)S(1)} %fusion.104), channel_id=1, source_target_pairs={{0,32},{32,64},{64,96},{96,128},{128,160},{160,192},{192,224},{224... | collective-permute-start | bytes 4616 | tf_op jit(solution)/shard_map/ppermute | solution.py:27
  15.9 1.9 collective-permute-start
  22.4 1.1 copy.49
  23.8 1.4 collective-permute-done
  27.0 1.3 dynamic-slice
  29.2 36.4 %all-reduce.1 = bf16[128]{0:T(256)(128)(2,1)S(1)} all-reduce(bf16[128]{0:T(256)(128)(2,1)S(1)} %dynamic-update-slice), channel_id=2, replica_groups=mesh['ctx'=16,'head'=32] {'ctx'}, use_global_device_ids=true, to_apply=%add.1 | all-reduce | flops 128 | bytes 512
  66.5 34.1 %all-gather.6.cloned.1.call-done = bf16[2,4096,128]{2,1,0:T(8,128)(2,1)} async-done(((bf16[2,256,128]{2,1,0:T(8,128)(2,1)}), bf16[2,4096,128]{2,1,0:T(8,128)(2,1)}) %all-gather.6.cloned.1.call-update) | async-done | bytes 2097168 | tf_op jit(solution)/shard_map/all_gather | solution.py:144
  100.7 9.5 %conditional.1 = (f32[2,256]{1,0:T(2,128)S(1)}, f32[2,256,128]{2,1,0:T(8,128)S(1)}) conditional(s32[]{:T(128)} %convert_element_type.138, () %tuple.24, (s32[]{:T(128)}, s32[256]{0:T(256)S(1)}, bf16[2,4096,128]{2,1,0:T(8,128)(2,1)}, bf16[256,256]{1,0:T(8,128)(2,1)S(1)}) %tuple.76), branch_computations={%region_7.8_spmd, %region_8.17_spmd} | conditional | flops 1102521088 | bytes 42316848 | solution.py:173
  101.7 1.4 fusion
  104.5 1.1 fusion.5
  105.6 1.1 fusion.9
  111.0 81.5 %all-gather.4.cloned.1.call-done = bf16[16,8,64,128]{3,2,1,0:T(8,128)(2,1)} async-done(((bf16[1,8,64,128]{3,2,1,0:T(8,128)(2,1)}), bf16[16,8,64,128]{3,2,1,0:T(8,128)(2,1)}) %all-gather.4.cloned.1.call-update) | async-done | bytes 2097168 | tf_op jit(solution)/shard_map/all_gather | solution.py:33
  192.5 14.9 %while.12 = (s32[]{:T(128)}, f32[8,64,128]{2,1,0:T(8,128)S(1)}, s32[]{:T(128)}, bf16[16,8]{1,0:T(8,128)(2,1)S(1)}, bf16[16,8,64,128]{3,2,1,0:T(8,128)(2,1)}, /*index=5*/s32[]{:T(128)}, s32[]{:T(128)}, s32[]{:T(128)}) while((s32[]{:T(128)}, f32[8,64,128]{2,1,0:T(8,128)S(1)}, s32[]{:T(128)}, bf16[16,8]{1,0:T(8,128)(2,1)S(1)}, ...), condition=%wide.region_4.5_spmd, body=%wide.region_3.4_spmd.sunk | while | flops 196621 | bytes 655567 | solution.py:47
  192.6 1.0 convert_add_fusion.2
  193.6 1.0 convert_add_fusion.2
  194.7 1.0 convert_add_fusion.2
  195.7 1.0 convert_add_fusion.2
  196.8 1.0 convert_add_fusion.2
  198.9 1.0 convert_add_fusion.2
  200.0 1.0 convert_add_fusion.2
  201.1 1.0 convert_add_fusion.2
  202.1 1.0 convert_add_fusion.2
  208.7 54.0 %psum.7 = f32[8,256]{1,0:T(8,128)S(1)} all-reduce(f32[8,256]{1,0:T(8,128)S(1)} %broadcast_select_fusion), channel_id=1, replica_groups=mesh['ctx'=16,'head'=32] {'head'}, use_global_device_ids=true, to_apply=%region_6.7 | all-reduce | flops 2048 | bytes 16384 | tf_op jit(solution)/shard_map/psum | solution.py:125
  (90 shorter events, 24.5 us)
Async XLA Ops:
  7.2 1.2 copy-start
  7.2 93.5 %all-gather.6.cloned.1.call-start = ((), (), s32[]{:S(2)}) async-start(), calls=%async_computation.1 | async-start | bytes 2228224 | tf_op jit(solution)/shard_map/all_gather | solution.py:144
  9.1 183.4 %all-gather.4.cloned.1.call-start = ((), (), s32[]{:S(2)}) async-start(), calls=%async_computation | async-start | bytes 2228224 | tf_op jit(solution)/shard_map/all_gather | solution.py:33
  10.1 13.4 %collective-permute-start.1 = (bf16[3,256]{1,0:T(4,128)(2,1)S(1)}, bf16[3,256]{1,0:T(4,128)(2,1)S(1)}, u32[]{:S(2)}, u32[]{:S(2)}) collective-permute-start(bf16[3,256]{1,0:T(4,128)(2,1)S(1)} %fusion.104), channel_id=1, source_target_pairs={{0,32},{32,64},{64,96},{96,128},{128,160},{160,192},{192,224},{224... | collective-permute-start | bytes 4616 | tf_op jit(solution)/shard_map/ppermute | solution.py:27
  15.9 9.3 %collective-permute-start = (bf16[3,512]{0,1:T(8,128)(2,1)S(1)}, bf16[3,512]{0,1:T(8,128)(2,1)S(1)}, u32[]{:S(2)}, u32[]{:S(2)}) collective-permute-start(bf16[3,512]{0,1:T(8,128)(2,1)S(1)} %copy.48), channel_id=1, source_target_pairs={{0,32},{32,64},{64,96},{96,128},{128,160},{160,192},{192,224},{224... | collective-permute-start | bytes 9224 | tf_op jit(solution)/shard_map/ppermute | solution.py:27
  23.6 42.1 %copy-start.1 = (bf16[256,512]{1,0:T(8,128)(2,1)S(1)}, bf16[256,512]{1,0:T(8,128)(2,1)}, u32[]{:S(2)}) copy-start(bf16[256,512]{1,0:T(8,128)(2,1)} %param.16) | copy-start | bytes 786436
  26.2 74.5 %copy-start.5 = (bf16[256,256]{1,0:T(8,128)(2,1)S(1)}, bf16[256,256]{1,0:T(8,128)(2,1)}, u32[]{:S(2)}) copy-start(bf16[256,256]{1,0:T(8,128)(2,1)} %param.24) | copy-start | bytes 393220
  100.7 2.4 copy-start.4
  110.2 97.2 %copy-start.3 = (f32[8]{0:T(128)S(1)}, f32[8]{0:T(128)}, u32[]{:S(2)}) copy-start(f32[8]{0:T(128)} %param.20) | copy-start | bytes 100
  207.4 55.3 %copy-start.2 = (f32[512]{0:T(512)S(1)}, f32[512]{0:T(512)}, u32[]{:S(2)}) copy-start(f32[512]{0:T(512)} %param.23) | copy-start | bytes 6148
Sparse Core Ops, SparseCore 0:
  11.8 88.8 all-gather.5
  104.4 88.0 all-gather.3
where the time goes:
time: 271 us
  waiting for transfers between devices  117 us (43%)
  blocking collectives  90.3 us (33%)
  other arithmetic  24.5 us (9%)
  between operations  15 us (6%)
  local copies, waits for them, and re-layouts  8.53 us (3%)
  matrix products  7.67 us (3%)
  starting transfers between devices  6.93 us (3%)
    all_gather x1, waiting for transfers between devices, carried_in(): lax.all_gather(a.astype(kind), axis)  81.5 us
    psum x1, blocking collectives, local(): summed = lax.psum(group_stat, 'head')  54 us
    unnamed x1, blocking collectives  36.4 us
    all_gather x1, waiting for transfers between devices, local(): piece = lax.all_gather(kv_mine, 'ctx', axis=1, tiled=True)  34.1 us
    add x14, other arithmetic, combine(): jnp.exp(later[0])[:, None, None] * earlier[1] + later[1]  14.3 us
    ppermute x2, starting transfers between devices, from_behind(): return lax.ppermute(x, axis, pairs)  6.85 us
  transfers between devices with their start and end apart: 4, of which 3 were waited for; matrix products, arithmetic and copies ran while one was open for 8% of the time, Pallas kernels for 0%

commit v1 on v0

v1 whole, which is shorter than its diff:
```python
import functools
import math

import jax
import jax.numpy as jnp
from jax import lax
from jax.experimental import pallas as pl
from jax.experimental.pallas import tpu as pltpu
from jax.sharding import PartitionSpec as P

GROUPS = 8
STATE = 128
HEAD_DIM = 128
CONV = 4
TOK = 256
HEADS = 8
CHAN = 512
N_CTX = 16
ROWS_Z = 8
HALF = CHAN // 2
SLICE = 16
QUART = TOK // 4
EPSILON = 1e-05
NEGATIVE = -1e30
HIGH = lax.Precision.HIGHEST
MESH = pl.DeviceIdType.MESH
F32 = jnp.float32
BF16 = jnp.bfloat16
PEERS = ((0, 1), (1, 0), (1, 1))
EXP_SCALE = math.log2(math.e) / math.sqrt(HEAD_DIM)


def silu(v):
    return v / (1.0 + jnp.exp(-v))


def conv_rows(pad_ref, taps, cols):
    total = jnp.zeros((TOK, cols.size), F32)
    for k in range(CONV):
        total = total + pad_ref[5 + k : 5 + k + TOK, cols] * taps[k : k + 1]
    return silu(total)


def kernel(
    x_hbm, z_hbm, bc_hbm, dt_ref, alog_ref, dskip_ref, cx_ref, cbc_ref, gain_ref, q_hbm, kv_hbm,
    ssm_ref, attn_ref,
    x_v, z_v, b_v, c_v, q_v, q2_v, kvbuf, halo_x, halo_bc, pad_x, pad_bc,
    st_send, in_a, out_b, in_b, dec_send, dec_in, pre_v, sz_v, ecx_v, cb_v, sq_v,
    m_v, l_v, o_v,
    loc, h_s, h_r, d_s, d_r, a_s, a_r, b_s, b_r, q_s, q_r, s1_s, s1_r, x_s, x_r, c_s, c_r,
):
    c = lax.axis_index("ctx")
    hd = lax.axis_index("head")
    z, xh = lax.div(c, 2), lax.rem(c, 2)
    y, qi = lax.div(hd, 4), lax.rem(hd, 4)
    xl, core = lax.div(qi, 2), lax.rem(qi, 2)
    flip_c = 1 - 2 * xh
    flip_l = 2 * (1 - 2 * xl)
    sib = hd + 1 - 2 * core
    ycol = pl.multiple_of(y * 128, 128)
    ycol2 = pl.multiple_of(GROUPS * STATE + y * 128, 128)

    def remote(src, dst, ss, rs, ctx, head):
        return pltpu.make_async_remote_copy(
            src_ref=src, dst_ref=dst, send_sem=ss, recv_sem=rs,
            device_id=(ctx, head), device_id_type=MESH,
        )

    loads = [
        pltpu.make_async_copy(x_hbm, x_v, loc.at[0]),
        pltpu.make_async_copy(bc_hbm.at[:, pl.ds(ycol, 128)], b_v, loc.at[1]),
        pltpu.make_async_copy(bc_hbm.at[:, pl.ds(ycol2, 128)], c_v, loc.at[2]),
        pltpu.make_async_copy(q_hbm, q_v, loc.at[3]),
        pltpu.make_async_copy(z_hbm, z_v, loc.at[4]),
    ]
    for i in range(4):
        loads.append(
            pltpu.make_async_copy(
                kv_hbm.at[:, pl.ds(QUART * i, QUART), pl.ds(ycol, 128)],
                kvbuf.at[:, z, xh, i // 2, i % 2],
                loc.at[5 + i],
            )
        )
    for cp in loads:
        cp.start()

    barrier = pltpu.get_barrier_semaphore()

    def greet(ctx, head):
        pl.semaphore_signal(barrier, inc=1, device_id=(ctx, head), device_id_type=MESH)

    def greet_ctx(d, carry):
        greet(lax.rem(c + d, N_CTX), hd)
        return carry

    lax.fori_loop(1, N_CTX, greet_ctx, 0)
    greet(c, hd + flip_l)
    greet(c + flip_c, hd + flip_l)
    greet(c, sib)
    greet(c, sib + flip_l)

    a_log = jnp.zeros((HEADS, 1), F32)
    head_row = lax.broadcasted_iota(jnp.int32, (HEADS, 1), 0)
    for h in range(HEADS):
        a_log = jnp.where(head_row == h, alog_ref[h], a_log)
    step = jnp.log(1.0 + jnp.exp(dt_ref[...]))
    cum = -jnp.exp(a_log) * step
    lane = lax.broadcasted_iota(jnp.int32, (HEADS, TOK), 1)
    shift = 1
    while shift < TOK:
        cum = cum + jnp.where(lane >= shift, pltpu.roll(cum, shift, 1), 0.0)
        shift *= 2
    last = cum[:, TOK - 1 : TOK]
    of_head = (
        lax.div(lax.broadcasted_iota(jnp.int32, (HEADS, CHAN), 1), CHAN // HEADS)
        == lax.broadcasted_iota(jnp.int32, (HEADS, CHAN), 0)
    )
    spread = jnp.where(of_head, 1.0, 0.0).astype(F32)
    total_row = jnp.sum(jnp.where(of_head, last, 0.0), axis=0, keepdims=True)
    for half in range(2):
        dec_send[half] = total_row[:, half * HALF : (half + 1) * HALF]
    own_half = lax.div(c, 8)

    pl.semaphore_wait(barrier, N_CTX - 1 + 4)

    def halo_copies():
        nxt = lax.rem(c + 1, N_CTX)
        tail = pl.ds(TOK - 16, 16)
        return [
            remote(x_hbm.at[tail, :], halo_x, h_s.at[0], h_r.at[0], nxt, hd),
            remote(bc_hbm.at[tail, pl.ds(ycol, 128)], halo_bc.at[0], h_s.at[1], h_r.at[1], nxt, hd),
            remote(bc_hbm.at[tail, pl.ds(ycol2, 128)], halo_bc.at[1], h_s.at[2], h_r.at[2], nxt, hd),
        ]

    @pl.when(c < N_CTX - 1)
    def _():
        for cp in halo_copies():
            cp.start()

    def dec_copy(d):
        to = lax.rem(c + d, N_CTX)
        return remote(dec_send.at[lax.div(to, 8)], dec_in.at[c], d_s.at[d], d_r.at[d], to, hd)

    def dec_start(d, carry):
        dec_copy(d).start()
        return carry

    lax.fori_loop(1, N_CTX, dec_start, 0)
    dec_in[c] = dec_send[own_half]

    def kv1_copy(d):
        return remote(
            kv_hbm.at[:, pl.ds(pl.multiple_of(QUART * qi, QUART), QUART), pl.ds(ycol, 128)],
            kvbuf.at[:, z, xh, xl, core],
            s1_s.at[d], s1_r.at[d], lax.rem(c + 2 * d, N_CTX), hd,
        )

    def kv1_start(d, carry):
        kv1_copy(d).start()
        return carry

    lax.fori_loop(1, ROWS_Z - z, kv1_start, 0)

    def x_copy(d, p):
        fh, fl = PEERS[p]
        piece = kvbuf.at[:, z - d, xh, xl, core]
        return remote(piece, piece, x_s.at[d, p], x_r.at[d, p], c + fh * flip_c, hd + fl * flip_l)

    def core_copy(d):
        piece = kvbuf.at[:, z - d, :, :, core]
        return remote(piece, piece, c_s.at[d], c_r.at[d], c, sib)

    def core_copy_own():
        piece = kvbuf.at[:, z, 1 - xh, :, core]
        return remote(piece, piece, c_s.at[0], c_r.at[0], c, sib)

    for i in range(4):
        loads[5 + i].wait()
    for p in (1, 2):
        x_copy(0, p).start()

    loads[3].wait()
    q2_v[0:TOK] = q_v[:, :HEAD_DIM]
    q2_v[TOK:] = q_v[:, HEAD_DIM:]

    def attend(keys, values, mask, first):
        logits = lax.dot_general(
            keys, q2_v[...], (((1,), (1,)), ((), ())), preferred_element_type=F32
        )
        if mask is not None:
            logits = jnp.where(mask, logits, NEGATIVE)
        top = jnp.max(logits, axis=0, keepdims=True)
        if not first:
            top = jnp.maximum(m_v[...], top)
        grown = jnp.exp2((logits - top) * EXP_SCALE)
        if mask is not None:
            grown = jnp.where(mask, grown, 0.0)
        den = jnp.sum(grown, axis=0, keepdims=True)
        got = jnp.dot(values.T, grown.astype(BF16), preferred_element_type=F32)
        if first:
            l_v[...] = den
            o_v[...] = got
        else:
            shrink = jnp.exp2((m_v[...] - top) * EXP_SCALE)
            l_v[...] = l_v[...] * shrink + den
            o_v[...] = o_v[...] * shrink + got
        m_v[...] = top

    key_at = lax.broadcasted_iota(jnp.int32, (TOK, 2 * TOK), 0)
    query_at = lax.rem(lax.broadcasted_iota(jnp.int32, (TOK, 2 * TOK), 1), TOK)
    attend(
        kvbuf[0, z, xh].reshape(TOK, HEAD_DIM), kvbuf[1, z, xh].reshape(TOK, HEAD_DIM),
        key_at <= query_at, True,
    )

    loads[0].wait()
    loads[1].wait()
    loads[2].wait()

    @pl.when(c > 0)
    def _():
        for cp in halo_copies():
            cp.wait_recv()

    @pl.when(c == 0)
    def _():
        halo_x[...] = jnp.zeros_like(halo_x)
        halo_bc[...] = jnp.zeros_like(halo_bc)

    pad_bc[8:, 0:STATE] = b_v[...].astype(F32)
    pad_bc[8:, STATE:] = c_v[...].astype(F32)
    pad_bc[0:8, 0:STATE] = halo_bc[0].astype(F32)[8:16]
    pad_bc[0:8, STATE:] = halo_bc[1].astype(F32)[8:16]
    pad_x[8:] = x_v[...].astype(F32)
    pad_x[0:8] = halo_x[...].astype(F32)[8:16]
    b_conv = conv_rows(pad_bc, cbc_ref[:, pl.ds(ycol, 128)].astype(F32), pl.ds(0, STATE))
    b_t = b_conv.T.astype(BF16)
    c_conv = conv_rows(pad_bc, cbc_ref[:, pl.ds(ycol2, 128)].astype(F32), pl.ds(STATE, STATE))
    cb_v[...] = c_conv.astype(BF16)
    x_conv = conv_rows(pad_x, cx_ref[...].astype(F32), pl.ds(0, CHAN)).astype(BF16)
    x_v[...] = x_conv
    wide_x = x_conv.astype(F32)

    tail = jnp.exp(last - cum) * step
    tail_x = jnp.dot(tail.T, spread, precision=HIGH, preferred_element_type=F32)
    carried = (tail_x * wide_x).astype(BF16)
    state = jnp.dot(b_t, carried, preferred_element_type=F32).astype(BF16)
    for half in range(2):
        st_send[8 * half : 8 * half + 8] = state[:, half * HALF : (half + 1) * HALF].reshape(
            8, SLICE, HALF
        )

    def a_copy(d):
        to = lax.rem(c + d, N_CTX)
        return remote(st_send.at[to], in_a.at[c], a_s.at[d], a_r.at[d], to, hd)

    def a_start(d, carry):
        a_copy(d).start()
        return carry

    lax.fori_loop(1, N_CTX, a_start, 0)
    in_a[c] = st_send[c]

    def forward(d, carry):
        kv1_copy(d).wait_recv()
        for p in range(3):
            x_copy(d, p).start()
        return carry

    lax.fori_loop(1, z + 1, forward, 0)

    scores = jnp.dot(cb_v[...], b_t, preferred_element_type=F32)
    t_at = lax.broadcasted_iota(jnp.int32, (TOK, TOK), 0)
    s_at = lax.broadcasted_iota(jnp.int32, (TOK, TOK), 1)
    scores = jnp.where(s_at <= t_at, scores, 0.0)
    cum_t = cum.T
    skip_row = jnp.zeros((1, CHAN), F32)
    head_of_lane = lax.div(lax.broadcasted_iota(jnp.int32, (1, CHAN), 1), CHAN // HEADS)
    for h in range(HEADS):
        skip_row = jnp.where(head_of_lane == h, dskip_ref[h], skip_row)
    left = lax.broadcasted_iota(jnp.int32, (TOK, 128), 1) < 64
    for pair in range(HEADS // 2):
        cols = slice(128 * pair, 128 * pair + 128)
        both = []
        for h in (2 * pair, 2 * pair + 1):
            gap = jnp.minimum(cum_t[:, h : h + 1] - cum[h : h + 1, :], 0.0)
            weights = (scores * jnp.exp(gap) * step[h : h + 1, :]).astype(BF16)
            both.append(jnp.dot(weights, x_v[:, cols], preferred_element_type=F32))
        pre_v[:, cols] = (
            jnp.where(left, both[0], both[1])
            + skip_row[:, cols] * x_v[:, cols].astype(F32)
        )
    ecx_v[...] = jnp.dot(jnp.exp(cum).T, spread, precision=HIGH, preferred_element_type=F32)
    loads[4].wait()
    sz_v[...] = silu(z_v[...].astype(F32))

    def a_wait(d, carry):
        dec_copy(d).wait_recv()
        a_copy(d).wait_recv()
        return carry

    lax.fori_loop(1, N_CTX, a_wait, 0)
    running = jnp.zeros((SLICE, HALF), F32)
    for k in range(N_CTX):
        out_b[k] = running.astype(BF16)
        running = jnp.exp(dec_in[k]) * running + in_a[k].astype(F32)

    def b_copy(d):
        to = lax.rem(c + d, N_CTX)
        return remote(out_b.at[to], in_b.at[c], b_s.at[d], b_r.at[d], to, hd)

    def b_start(d, carry):
        b_copy(d).start()
        return carry

    lax.fori_loop(1, N_CTX, b_start, 0)
    in_b[c] = out_b[c]

    for p in (1, 2):
        x_copy(0, p).wait_recv()
    core_copy_own().start()

    def to_core(d, carry):
        for p in range(3):
            x_copy(d, p).wait_recv()
        core_copy(d).start()
        return carry

    lax.fori_loop(1, z + 1, to_core, 0)

    def b_wait(d, carry):
        b_copy(d).wait_recv()
        return carry

    lax.fori_loop(1, N_CTX, b_wait, 0)
    squares = jnp.zeros((TOK, 128), F32)
    for half in range(2):
        cols = slice(half * HALF, (half + 1) * HALF)
        entering = in_b[8 * half : 8 * half + 8].reshape(STATE, HALF)
        reach = jnp.dot(cb_v[...], entering, preferred_element_type=F32)
        gated = (pre_v[:, cols] + ecx_v[:, cols] * reach) * sz_v[:, cols]
        pre_v[:, cols] = gated
        squares = squares + gated[:, :128] * gated[:, :128] + gated[:, 128:] * gated[:, 128:]
    sq_v[0] = jnp.sum(squares.T, axis=0, keepdims=True)

    def quad_copies():
        return [
            remote(sq_v.at[0], sq_v.at[1], q_s.at[0], q_r.at[0], c, sib),
            remote(sq_v.at[0], sq_v.at[2], q_s.at[1], q_r.at[1], c, hd + flip_l),
            remote(sq_v.at[0], sq_v.at[3], q_s.at[2], q_r.at[2], c, sib + flip_l),
        ]

    for cp in quad_copies():
        cp.start()

    core_copy_own().wait_recv()

    @pl.when(xh == 1)
    def _():
        attend(
            kvbuf[0, z, 0].reshape(TOK, HEAD_DIM), kvbuf[1, z, 0].reshape(TOK, HEAD_DIM),
            None, False,
        )

    def attend_row(d, carry):
        core_copy(d).wait_recv()
        attend(
            kvbuf[0, z - d].reshape(2 * TOK, HEAD_DIM), kvbuf[1, z - d].reshape(2 * TOK, HEAD_DIM),
            None, False,
        )
        return carry

    lax.fori_loop(1, z + 1, attend_row, 0)
    result = o_v[...] / l_v[...]
    for h in range(2):
        attn_ref[:, h * HEAD_DIM : (h + 1) * HEAD_DIM] = result[
            :, h * TOK : (h + 1) * TOK
        ].T.astype(BF16)

    for cp in quad_copies():
        cp.wait_recv()
    group_total = sq_v[0] + sq_v[1] + sq_v[2] + sq_v[3]
    scale = lax.rsqrt(group_total * (1.0 / 2048.0) + EPSILON)
    scale_col = jnp.broadcast_to(scale, (8, TOK)).T[:, 0:1]
    ssm_ref[...] = (pre_v[...] * scale_col * gain_ref[...]).astype(BF16)

    @pl.when(c < N_CTX - 1)
    def _():
        for cp in halo_copies():
            cp.wait_send()

    def sent(d, carry):
        dec_copy(d).wait_send()
        a_copy(d).wait_send()
        b_copy(d).wait_send()
        return carry

    lax.fori_loop(1, N_CTX, sent, 0)

    def kv1_sent(d, carry):
        kv1_copy(d).wait_send()
        return carry

    lax.fori_loop(1, ROWS_Z - z, kv1_sent, 0)

    def row_sent(d, carry):
        for p in range(3):
            x_copy(d, p).wait_send()
        core_copy(d).wait_send()
        return carry

    lax.fori_loop(1, z + 1, row_sent, 0)
    for p in (1, 2):
        x_copy(0, p).wait_send()
    core_copy_own().wait_send()
    for cp in quad_copies():
        cp.wait_send()


def local(
    x_in, z_in, bc_in, dt_raw, a_log, d_skip, conv_x, conv_bc, norm_gain, queries, keys_values
):
    any_spec = pl.BlockSpec(memory_space=pl.ANY)
    vmem = pl.BlockSpec(memory_space=pltpu.VMEM)
    smem = pl.BlockSpec(memory_space=pltpu.SMEM)
    dma = pltpu.SemaphoreType.DMA
    return pl.pallas_call(
        kernel,
        out_shape=(
            jax.ShapeDtypeStruct((TOK, CHAN), BF16),
            jax.ShapeDtypeStruct((TOK, 2 * HEAD_DIM), BF16),
        ),
        in_specs=[
            any_spec, any_spec, any_spec, vmem, smem, smem, vmem, vmem, vmem, any_spec, any_spec,
        ],
        out_specs=(vmem, vmem),
        scratch_shapes=[
            pltpu.VMEM((TOK, CHAN), BF16),
            pltpu.VMEM((TOK, CHAN), BF16),
            pltpu.VMEM((TOK, STATE), BF16),
            pltpu.VMEM((TOK, STATE), BF16),
            pltpu.VMEM((TOK, 2 * HEAD_DIM), BF16),
            pltpu.VMEM((2 * TOK, HEAD_DIM), BF16),
            pltpu.VMEM((2, ROWS_Z, 2, 2, 2, QUART, HEAD_DIM), BF16),
            pltpu.VMEM((16, CHAN), BF16),
            pltpu.VMEM((2, 16, STATE), BF16),
            pltpu.VMEM((8 + TOK, CHAN), F32),
            pltpu.VMEM((8 + TOK, 2 * STATE), F32),
            pltpu.VMEM((N_CTX, SLICE, HALF), BF16),
            pltpu.VMEM((N_CTX, SLICE, HALF), BF16),
            pltpu.VMEM((N_CTX, SLICE, HALF), BF16),
            pltpu.VMEM((N_CTX, SLICE, HALF), BF16),
            pltpu.VMEM((2, 1, HALF), F32),
            pltpu.VMEM((N_CTX, 1, HALF), F32),
            pltpu.VMEM((TOK, CHAN), F32),
            pltpu.VMEM((TOK, CHAN), F32),
            pltpu.VMEM((TOK, CHAN), F32),
            pltpu.VMEM((TOK, STATE), BF16),
            pltpu.VMEM((4, 1, TOK), F32),
            pltpu.VMEM((1, 2 * TOK), F32),
            pltpu.VMEM((1, 2 * TOK), F32),
            pltpu.VMEM((HEAD_DIM, 2 * TOK), F32),
            dma((9,)), dma((3,)), dma((3,)),
            dma((N_CTX,)), dma((N_CTX,)), dma((N_CTX,)), dma((N_CTX,)),
            dma((N_CTX,)), dma((N_CTX,)),
            dma((3,)), dma((3,)), dma((ROWS_Z,)), dma((ROWS_Z,)),
            dma((ROWS_Z, 3)), dma((ROWS_Z, 3)), dma((ROWS_Z,)), dma((ROWS_Z,)),
        ],
        compiler_params=pltpu.CompilerParams(
            collective_id=0, has_side_effects=True, vmem_limit_bytes=40 * 1024 * 1024
        ),
        name="mixer",
    )(
        x_in, z_in, bc_in, dt_raw, a_log, d_skip, conv_x, conv_bc,
        norm_gain.reshape(1, CHAN), queries, keys_values,
    )


def solution(mesh):
    placed = (
        P("ctx", "head"),
        P("ctx", "head"),
        P("ctx", None),
        P("head", "ctx"),
        P("head"),
        P("head"),
        P(None, "head"),
        P(),
        P("head"),
        P("ctx", "head"),
        P(None, "ctx", None),
    )
    return jax.shard_map(
        local,
        mesh=mesh,
        in_specs=placed,
        out_specs=(P("ctx", "head"), P("ctx", "head")),
        check_vma=False,
    )
```

time: 271 us -> 50.6 us (0.19)
  the two profiles are of different devices: /device:TPU:448 before, /device:TPU:1 now
where the time goes in v1:
time: 50.6 us; the launch traced here: 50.1 us
  Pallas kernels  39.4 us (78%)
  local copies, waits for them, and re-layouts  10 us (20%)
  between operations  0.67 us (1%)
    pallas_call x1, Pallas kernels, local(): pl.pallas_call(kernel, out_shape=(jax.ShapeDtypeStruct((TOK, CHAN), BF16)...  39.4 us
    unnamed x24, local copies, waits for them, and re-layouts  10 us

profile of v1, /device:TPU:1, one launch (start us, length us, event | category | flops | bytes accessed | tf_op | source)
XLA Modules:
  0.0 50.1 jit_solution(432601797567936364)
XLA Ops:
  0.6 0.0 copy-start.10
  0.6 0.0 copy-start.9
  0.7 0.6 %copy-done.10 = f32[8]{0:T(128)S(1)} copy-done((f32[8]{0:T(128)S(1)}, f32[8]{0:T(128)}, u32[]{:S(2)}) %copy-start.10) | copy-done | bytes 56
  1.3 0.0 copy-done.9
  1.3 0.0 copy-start
  1.3 1.2 %copy-done = bf16[256,2048]{1,0:T(8,128)(2,1)S(1)} copy-done((bf16[256,2048]{1,0:T(8,128)(2,1)S(1)}, bf16[256,2048]{1,0:T(8,128)(2,1)}, u32[]{:S(2)}) %copy-start) | copy-done | bytes 1048600
  2.5 0.0 copy-start.1
  2.5 1.2 %copy-done.1 = bf16[2,256,1024]{2,1,0:T(8,128)(2,1)S(1)} copy-done((bf16[2,256,1024]{2,1,0:T(8,128)(2,1)S(1)}, bf16[2,256,1024]{2,1,0:T(8,128)(2,1)}, u32[]{:S(2)}) %copy-start.1) | copy-done | bytes 1048600
  3.8 0.0 copy-start.2
  3.8 0.9 %copy-done.2 = bf16[256,512]{1,0:T(8,128)(2,1)S(1)} copy-done((bf16[256,512]{1,0:T(8,128)(2,1)S(1)}, bf16[256,512]{1,0:T(8,128)(2,1)}, u32[]{:S(2)}) %copy-start.2) | copy-done | bytes 262168
  4.7 0.0 copy-start.3
  4.7 0.9 %copy-done.3 = bf16[256,512]{1,0:T(8,128)(2,1)S(1)} copy-done((bf16[256,512]{1,0:T(8,128)(2,1)S(1)}, bf16[256,512]{1,0:T(8,128)(2,1)}, u32[]{:S(2)}) %copy-start.3) | copy-done | bytes 262168
  5.7 0.0 copy-start.4
  5.7 0.9 %copy-done.4 = bf16[256,256]{1,0:T(8,128)(2,1)S(1)} copy-done((bf16[256,256]{1,0:T(8,128)(2,1)S(1)}, bf16[256,256]{1,0:T(8,128)(2,1)}, u32[]{:S(2)}) %copy-start.4) | copy-done | bytes 131096
  6.6 0.0 copy-start.5
  6.6 0.7 %copy-done.5 = bf16[4,2048]{1,0:T(4,128)(2,1)S(1)} copy-done((bf16[4,2048]{1,0:T(4,128)(2,1)S(1)}, bf16[4,2048]{1,0:T(4,128)(2,1)}, u32[]{:S(2)}) %copy-start.5) | copy-done | bytes 16408
  7.3 0.0 copy-start.6
  7.3 0.7 %copy-done.6 = f32[8,256]{1,0:T(8,128)S(1)} copy-done((f32[8,256]{1,0:T(8,128)S(1)}, f32[8,256]{1,0:T(8,128)}, u32[]{:S(2)}) %copy-start.6) | copy-done | bytes 8216
  8.0 0.0 copy-start.7
  8.0 0.7 %copy-done.7 = bf16[4,512]{1,0:T(4,128)(2,1)S(1)} copy-done((bf16[4,512]{1,0:T(4,128)(2,1)S(1)}, bf16[4,512]{1,0:T(4,128)(2,1)}, u32[]{:S(2)}) %copy-start.7) | copy-done | bytes 4120
  8.7 0.7 %copy-done.8 = f32[512]{0:T(512)S(1)} copy-done((f32[512]{0:T(512)S(1)}, f32[512]{0:T(512)}, u32[]{:S(2)}) %copy-start.8) | copy-done | bytes 2072
  9.3 39.4 %mixer.1 = (bf16[256,512]{1,0:T(8,128)(2,1)S(1)}, bf16[256,256]{1,0:T(8,128)(2,1)S(1)}) custom-call(bf16[256,512]{1,0:T(8,128)(2,1)S(1)} %copy-done.2, bf16[256,512]{1,0:T(8,128)(2,1)S(1)} %copy-done.3, bf16[256,2048]{1,0:T(8,128)(2,1)S(1)} %copy-done, f32[8,256]{1,0:T(8,128)S(1)} %copy-done.6, f32[8]{0:T(128)S(1)} %copy-done.9, f32[8]{0:T(128)S(1)} %copy-done.10, ...), custom_call_target="tpu_custom_call" | custom-call | tf_op jit(solution)/shard_map/mixer/pallas_call | solution.py:427
  48.8 0.7 %copy.15 = bf16[256,512]{1,0:T(8,128)(2,1)} copy(bf16[256,512]{1,0:T(8,128)(2,1)S(1)} %get-tuple-element.4) | data formatting | bytes 524288
  49.5 0.7 %copy.16 = bf16[256,256]{1,0:T(8,128)(2,1)} copy(bf16[256,256]{1,0:T(8,128)(2,1)S(1)} %get-tuple-element.5) | data formatting | bytes 262144
  (1 shorter events, 0.0 us)
Async XLA Ops:
  0.6 0.7 %copy-start.10 = (f32[8]{0:T(128)S(1)}, f32[8]{0:T(128)}, u32[]{:S(2)}) copy-start(f32[8]{0:T(128)} %dskip_ref.1) | copy-start | bytes 100
  0.6 0.7 %copy-start.9 = (f32[8]{0:T(128)S(1)}, f32[8]{0:T(128)}, u32[]{:S(2)}) copy-start(f32[8]{0:T(128)} %alog_ref.1) | copy-start | bytes 100
  1.3 1.2 %copy-start = (bf16[256,2048]{1,0:T(8,128)(2,1)S(1)}, bf16[256,2048]{1,0:T(8,128)(2,1)}, u32[]{:S(2)}) copy-start(bf16[256,2048]{1,0:T(8,128)(2,1)} %bc_hbm.1) | copy-start | bytes 3145732
  2.5 1.2 %copy-start.1 = (bf16[2,256,1024]{2,1,0:T(8,128)(2,1)S(1)}, bf16[2,256,1024]{2,1,0:T(8,128)(2,1)}, u32[]{:S(2)}) copy-start(bf16[2,256,1024]{2,1,0:T(8,128)(2,1)} %kv_hbm.1) | copy-start | bytes 3145732
  3.8 0.9 %copy-start.2 = (bf16[256,512]{1,0:T(8,128)(2,1)S(1)}, bf16[256,512]{1,0:T(8,128)(2,1)}, u32[]{:S(2)}) copy-start(bf16[256,512]{1,0:T(8,128)(2,1)} %x_hbm.1) | copy-start | bytes 786436
  4.7 0.9 %copy-start.3 = (bf16[256,512]{1,0:T(8,128)(2,1)S(1)}, bf16[256,512]{1,0:T(8,128)(2,1)}, u32[]{:S(2)}) copy-start(bf16[256,512]{1,0:T(8,128)(2,1)} %z_hbm.1) | copy-start | bytes 786436
  5.7 0.9 %copy-start.4 = (bf16[256,256]{1,0:T(8,128)(2,1)S(1)}, bf16[256,256]{1,0:T(8,128)(2,1)}, u32[]{:S(2)}) copy-start(bf16[256,256]{1,0:T(8,128)(2,1)} %q_hbm.1) | copy-start | bytes 393220
  6.6 0.7 %copy-start.5 = (bf16[4,2048]{1,0:T(4,128)(2,1)S(1)}, bf16[4,2048]{1,0:T(4,128)(2,1)}, u32[]{:S(2)}) copy-start(bf16[4,2048]{1,0:T(4,128)(2,1)} %cbc_ref.1) | copy-start | bytes 49156
  7.3 0.7 %copy-start.6 = (f32[8,256]{1,0:T(8,128)S(1)}, f32[8,256]{1,0:T(8,128)}, u32[]{:S(2)}) copy-start(f32[8,256]{1,0:T(8,128)} %dt_ref.1) | copy-start | bytes 24580
  8.0 0.7 %copy-start.7 = (bf16[4,512]{1,0:T(4,128)(2,1)S(1)}, bf16[4,512]{1,0:T(4,128)(2,1)}, u32[]{:S(2)}) copy-start(bf16[4,512]{1,0:T(4,128)(2,1)} %cx_ref.1) | copy-start | bytes 12292
  8.7 0.7 %copy-start.8 = (f32[512]{0:T(512)S(1)}, f32[512]{0:T(512)}, u32[]{:S(2)}) copy-start(f32[512]{0:T(512)} %param.19) | copy-start | bytes 6148

commit v2 on v1

v2 whole, which is shorter than its diff:
```python
import functools
import math

import jax
import jax.numpy as jnp
from jax import lax
from jax.experimental import pallas as pl
from jax.experimental.pallas import tpu as pltpu
from jax.sharding import PartitionSpec as P

GROUPS = 8
STATE = 128
HEAD_DIM = 128
CONV = 4
TOK = 256
HEADS = 8
CHAN = 512
N_CTX = 16
BLOCK = 128
ROWS_Z = 8
SLICE = STATE // 4
QUART = TOK // 4
EPSILON = 1e-05
NEGATIVE = -1e30
HIGH = lax.Precision.HIGHEST
MESH = pl.DeviceIdType.MESH
F32 = jnp.float32
BF16 = jnp.bfloat16
PEERS = ((0, 1), (1, 0), (1, 1))
EXP_SCALE = math.log2(math.e) / math.sqrt(HEAD_DIM)


def silu(v):
    return v / (1.0 + jnp.exp(-v))


def conv_rows(pad_ref, taps, cols, rows):
    total = jnp.zeros((rows, cols.size), F32)
    for k in range(CONV):
        total = total + pad_ref[5 + k : 5 + k + rows, cols] * taps[k : k + 1]
    return silu(total)


def kernel(
    x_hbm, z_hbm, bc_hbm, dt_hbm, alog_hbm, dskip_hbm, cx_hbm, cbc_hbm, gain_hbm, q_hbm, kv_hbm,
    ssm_hbm, attn_hbm,
    dt_ref, alog_ref, dskip_ref, cx_ref, cbc_ref, gain_ref,
    x_v, z_v, b_v, c_v, q_v, q2_v, kvbuf, halo_x, halo_bc, pad_x, pad_bc, bf_v,
    st_send, in_a, out_b, in_b, e_out, e_in, dec_send, dec_in, pre_v, sz_v, ecx_v, cb_v, sq_v,
    m_v, l_v, o_v, ssm_v, attn_v,
    loc, h_s, h_r, d_s, d_r, a_s, a_r, b_s, b_r, e_s, e_r, q_s, q_r, s1_s, s1_r,
    x_s, x_r, c_s, c_r, rdy,
):
    c = lax.axis_index("ctx")
    hd = lax.axis_index("head")
    z, xh = lax.div(c, 2), lax.rem(c, 2)
    grp, mem = lax.div(c, 4), lax.rem(c, 4)
    zodd = lax.rem(z, 2)
    y, qi = lax.div(hd, 4), lax.rem(hd, 4)
    xl, core = lax.div(qi, 2), lax.rem(qi, 2)
    flip_c = 1 - 2 * xh
    flip_l = 2 * (1 - 2 * xl)
    sib = hd + 1 - 2 * core
    ycol = pl.multiple_of(y * 128, 128)
    ycol2 = pl.multiple_of(GROUPS * STATE + y * 128, 128)
    mates = [lax.rem(mem + e, 4) for e in (1, 2, 3)]

    def remote(src, dst, ss, rs, ctx, head):
        return pltpu.make_async_remote_copy(
            src_ref=src, dst_ref=dst, send_sem=ss, recv_sem=rs,
            device_id=(ctx, head), device_id_type=MESH,
        )

    small = [
        pltpu.make_async_copy(src, dst, loc.at[i])
        for i, (src, dst) in enumerate(
            (
                (dt_hbm, dt_ref), (alog_hbm, alog_ref), (dskip_hbm, dskip_ref),
                (cx_hbm, cx_ref), (cbc_hbm, cbc_ref), (gain_hbm, gain_ref),
            )
        )
    ]
    load_x = pltpu.make_async_copy(x_hbm, x_v, loc.at[6])
    load_b = pltpu.make_async_copy(bc_hbm.at[:, pl.ds(ycol, 128)], b_v, loc.at[7])
    load_c = pltpu.make_async_copy(bc_hbm.at[:, pl.ds(ycol2, 128)], c_v, loc.at[8])
    load_q = pltpu.make_async_copy(q_hbm, q_v, loc.at[9])
    load_z = pltpu.make_async_copy(z_hbm, z_v, loc.at[10])
    load_kv = pltpu.make_async_copy(
        kv_hbm.at[:, :, :, :, pl.ds(ycol, 128)], kvbuf.at[:, z, xh], loc.at[11]
    )
    for cp in small + [load_b, load_c, load_x, load_kv, load_q, load_z]:
        cp.start()

    barrier = pltpu.get_barrier_semaphore()

    def greet(ctx, head):
        pl.semaphore_signal(barrier, inc=1, device_id=(ctx, head), device_id_type=MESH)

    for to in mates:
        greet(c - mem + to, hd)
    greet(c, sib)
    greet(c, hd + flip_l)
    greet(c, sib + flip_l)
    greet(c + flip_c, hd + flip_l)

    @pl.when((mem == 0) & (c > 0))
    def _():
        greet(c - 1, hd)

    def greet_later(d, carry):
        greet(c + 2 * d, hd)
        return carry

    lax.fori_loop(2 - zodd, ROWS_Z - z, greet_later, 0)

    for cp in small:
        cp.wait()
    a_log = jnp.zeros((HEADS, 1), F32)
    head_row = lax.broadcasted_iota(jnp.int32, (HEADS, 1), 0)
    for h in range(HEADS):
        a_log = jnp.where(head_row == h, alog_ref[h], a_log)
    step = jnp.log(1.0 + jnp.exp(dt_ref[...]))
    cum = -jnp.exp(a_log) * step
    lane = lax.broadcasted_iota(jnp.int32, (HEADS, TOK), 1)
    shift = 1
    while shift < TOK:
        cum = cum + jnp.where(lane >= shift, pltpu.roll(cum, shift, 1), 0.0)
        shift *= 2
    last = cum[:, TOK - 1 : TOK]
    of_head = (
        lax.div(lax.broadcasted_iota(jnp.int32, (HEADS, CHAN), 1), CHAN // HEADS)
        == lax.broadcasted_iota(jnp.int32, (HEADS, CHAN), 0)
    )
    spread = jnp.where(of_head, 1.0, 0.0).astype(F32)
    dec_send[...] = jnp.sum(jnp.where(of_head, last, 0.0), axis=0, keepdims=True)
    dec_in[mem] = dec_send[...]
    tail = jnp.exp(last - cum) * step
    tail_x = jnp.dot(tail.T, spread, precision=HIGH, preferred_element_type=F32)

    taps_b = cbc_ref[:, pl.ds(ycol, 128)].astype(F32)
    taps_c = cbc_ref[:, pl.ds(ycol2, 128)].astype(F32)
    taps_x = cx_ref[...].astype(F32)
    pad_bc[0:8] = jnp.zeros((8, 2 * STATE), F32)
    pad_x[0:8] = jnp.zeros((8, CHAN), F32)
    load_b.wait()
    load_c.wait()
    pad_bc[8:, 0:STATE] = b_v[...].astype(F32)
    pad_bc[8:, STATE:] = c_v[...].astype(F32)

    def convolve(rows):
        bf_v[0:rows] = conv_rows(pad_bc, taps_b, pl.ds(0, STATE), rows)
        cb_v[0:rows] = conv_rows(pad_bc, taps_c, pl.ds(STATE, STATE), rows).astype(BF16)
        x_v[0:rows] = conv_rows(pad_x, taps_x, pl.ds(0, CHAN), rows).astype(BF16)

    load_x.wait()
    pad_x[8:] = x_v[...].astype(F32)
    convolve(TOK)

    greeted = 3 + 4 + 2 * grp + jnp.where((mem == 3) & (c < N_CTX - 1), 1, 0)
    pl.semaphore_wait(barrier, greeted)

    def halo_copies():
        tail_rows = pl.ds(TOK - 16, 16)
        return [
            remote(x_hbm.at[tail_rows, :], halo_x, h_s.at[0], h_r.at[0], c + 1, hd),
            remote(
                bc_hbm.at[tail_rows, pl.ds(ycol, 128)], halo_bc.at[0],
                h_s.at[1], h_r.at[1], c + 1, hd,
            ),
            remote(
                bc_hbm.at[tail_rows, pl.ds(ycol2, 128)], halo_bc.at[1],
                h_s.at[2], h_r.at[2], c + 1, hd,
            ),
        ]

    @pl.when(c < N_CTX - 1)
    def _():
        for cp in halo_copies():
            cp.start()

    def dec_copy(to):
        return remote(dec_send, dec_in.at[mem], d_s, d_r, c - mem + to, hd)

    for to in mates:
        dec_copy(to).start()

    for far in (1, 2, 3):

        @pl.when(grp >= far)
        def _():
            for odd in range(2):
                pl.semaphore_signal(
                    rdy.at[far - 1], inc=1, device_id=(4 * (grp - far) + 2 * odd + xh, hd),
                    device_id_type=MESH,
                )

    def kv1_copy(d):
        return remote(
            kvbuf.at[:, z, xh, xl, core], kvbuf.at[:, z, xh, xl, core],
            s1_s.at[d], s1_r.at[d], c + 2 * d, hd,
        )

    def kv1_got(d):
        piece = kvbuf.at[:, z - d, xh, xl, core]
        return remote(piece, piece, s1_s.at[d], s1_r.at[d], c, sib)

    def kv1_group(far):
        @pl.when(grp + far < 4)
        def _():
            pl.semaphore_wait(rdy.at[far - 1], 2)
            for odd in range(2):
                kv1_copy(2 * far + odd - zodd).start()

    def x_copy(d, p):
        fh, fl = PEERS[p]
        piece = kvbuf.at[:, z - d, xh, xl, core]
        return remote(piece, piece, x_s.at[d, p], x_r.at[d, p], c + fh * flip_c, hd + fl * flip_l)

    def core_copy(d):
        piece = kvbuf.at[:, z - d, :, :, core]
        return remote(piece, piece, c_s.at[d], c_r.at[d], c, sib)

    def core_copy_own():
        piece = kvbuf.at[:, z, 1 - xh, :, core]
        return remote(piece, piece, c_s.at[0], c_r.at[0], c, sib)

    @pl.when(c > 0)
    def _():
        for cp in halo_copies():
            cp.wait_recv()
        pad_bc[0:8, 0:STATE] = halo_bc[0].astype(F32)[8:16]
        pad_bc[0:8, STATE:] = halo_bc[1].astype(F32)[8:16]
        pad_x[0:8] = halo_x[...].astype(F32)[8:16]
        convolve(16)

    b_t = bf_v[...].T.astype(BF16)
    carried = (tail_x * x_v[...].astype(F32)).astype(BF16)
    state = jnp.dot(b_t, carried, preferred_element_type=F32).astype(BF16)
    st_send[...] = state.reshape(4, SLICE, CHAN)

    def a_copy(to):
        return remote(st_send.at[to], in_a.at[mem], a_s, a_r, c - mem + to, hd)

    for to in mates:
        a_copy(to).start()
    in_a[mem] = st_send[mem]

    load_kv.wait()
    for p in (1, 2):
        x_copy(0, p).start()

    @pl.when(zodd == 0)
    def _():
        kv1_copy(1).start()

    kv1_group(1)

    scores = jnp.dot(cb_v[...], b_t, preferred_element_type=F32)
    t_at = lax.broadcasted_iota(jnp.int32, (TOK, TOK), 0)
    s_at = lax.broadcasted_iota(jnp.int32, (TOK, TOK), 1)
    scores = jnp.where(s_at <= t_at, scores, 0.0)
    cum_t = cum.T
    skip_row = jnp.zeros((1, CHAN), F32)
    head_of_lane = lax.div(lax.broadcasted_iota(jnp.int32, (1, CHAN), 1), CHAN // HEADS)
    for h in range(HEADS):
        skip_row = jnp.where(head_of_lane == h, dskip_ref[h], skip_row)
    left = lax.broadcasted_iota(jnp.int32, (BLOCK, 128), 1) < 64
    for low in (0, BLOCK):
        rows, upto = slice(low, low + BLOCK), low + BLOCK
        for pair in range(HEADS // 2):
            cols = slice(128 * pair, 128 * pair + 128)
            both = []
            for h in (2 * pair, 2 * pair + 1):
                gap = jnp.minimum(cum_t[rows, h : h + 1] - cum[h : h + 1, :upto], 0.0)
                weights = (scores[rows, :upto] * jnp.exp(gap) * step[h : h + 1, :upto]).astype(BF16)
                both.append(jnp.dot(weights, x_v[:upto, cols], preferred_element_type=F32))
            pre_v[rows, cols] = (
                jnp.where(left, both[0], both[1])
                + skip_row[:, cols] * x_v[rows, cols].astype(F32)
            )
    ecx_v[...] = jnp.dot(jnp.exp(cum).T, spread, precision=HIGH, preferred_element_type=F32)
    load_z.wait()
    sz_v[...] = silu(z_v[...].astype(F32))

    three = pl.ds(0, 3)

    def e_copy():
        return remote(e_out, e_in, e_s, e_r, c + 4, hd)

    remote(dec_in.at[three], dec_in.at[three], d_s, d_r, c, sib).wait_recv()
    remote(st_send.at[three], in_a.at[three], a_s, a_r, c, sib).wait_recv()

    @pl.when(grp > 0)
    def _():
        e_copy().wait_recv()

    @pl.when(grp == 0)
    def _():
        e_in[...] = jnp.zeros_like(e_in)

    running = e_in[...].astype(F32)
    for k in range(4):
        out_b[k] = running.astype(BF16)
        running = jnp.exp(dec_in[k]) * running + in_a[k].astype(F32)
    e_out[...] = running.astype(BF16)

    @pl.when(grp < 3)
    def _():
        e_copy().start()

    def b_copy(to):
        return remote(out_b.at[to], in_b.at[mem], b_s, b_r, c - mem + to, hd)

    for to in mates:
        b_copy(to).start()
    in_b[mem] = out_b[mem]

    kv1_group(2)

    for p in (1, 2):
        x_copy(0, p).wait_recv()
    core_copy_own().start()

    def forward(d, carry):
        kv1_got(d).wait_recv()
        for p in range(3):
            x_copy(d, p).start()
        return carry

    lax.fori_loop(1, z + 1, forward, 0)

    remote(out_b.at[three], in_b.at[three], b_s, b_r, c, sib).wait_recv()
    entering = in_b[...].reshape(STATE, CHAN)
    squares = jnp.zeros((TOK, 128), F32)
    for part in range(2):
        cols = slice(part * 256, (part + 1) * 256)
        reach = jnp.dot(cb_v[...], entering[:, cols], preferred_element_type=F32)
        gated = (pre_v[:, cols] + ecx_v[:, cols] * reach) * sz_v[:, cols]
        pre_v[:, cols] = gated
        squares = squares + gated[:, :128] * gated[:, :128] + gated[:, 128:] * gated[:, 128:]
    sq_v[0] = jnp.sum(squares.T, axis=0, keepdims=True)

    def quad_copies():
        return [
            remote(sq_v.at[0], sq_v.at[1], q_s.at[0], q_r.at[0], c, sib),
            remote(sq_v.at[0], sq_v.at[2], q_s.at[1], q_r.at[1], c, hd + flip_l),
            remote(sq_v.at[0], sq_v.at[3], q_s.at[2], q_r.at[2], c, sib + flip_l),
        ]

    for cp in quad_copies():
        cp.start()
    kv1_group(3)

    def attend(keys, values, mask, first):
        logits = lax.dot_general(
            keys, q2_v[...], (((1,), (1,)), ((), ())), preferred_element_type=F32
        )
        if mask is not None:
            logits = jnp.where(mask, logits, NEGATIVE)
        top = jnp.max(logits, axis=0, keepdims=True)
        if not first:
            top = jnp.maximum(m_v[...], top)
        grown = jnp.exp2((logits - top) * EXP_SCALE)
        if mask is not None:
            grown = jnp.where(mask, grown, 0.0)
        den = jnp.sum(grown, axis=0, keepdims=True)
        got = jnp.dot(values.T, grown.astype(BF16), preferred_element_type=F32)
        if first:
            l_v[...] = den
            o_v[...] = got
        else:
            shrink = jnp.exp2((m_v[...] - top) * EXP_SCALE)
            l_v[...] = l_v[...] * shrink + den
            o_v[...] = o_v[...] * shrink + got
        m_v[...] = top

    load_q.wait()
    q2_v[0:TOK] = q_v[:, :HEAD_DIM]
    q2_v[TOK:] = q_v[:, HEAD_DIM:]
    key_at = lax.broadcasted_iota(jnp.int32, (TOK, 2 * TOK), 0)
    query_at = lax.rem(lax.broadcasted_iota(jnp.int32, (TOK, 2 * TOK), 1), TOK)
    attend(
        kvbuf[0, z, xh].reshape(TOK, HEAD_DIM), kvbuf[1, z, xh].reshape(TOK, HEAD_DIM),
        key_at <= query_at, True,
    )
    core_copy_own().wait_recv()

    @pl.when(xh == 1)
    def _():
        attend(
            kvbuf[0, z, 0].reshape(TOK, HEAD_DIM), kvbuf[1, z, 0].reshape(TOK, HEAD_DIM),
            None, False,
        )

    for cp in quad_copies():
        cp.wait_recv()
    group_total = sq_v[0] + sq_v[1] + sq_v[2] + sq_v[3]
    scale = lax.rsqrt(group_total * (1.0 / 2048.0) + EPSILON)
    scale_col = jnp.broadcast_to(scale, (8, TOK)).T[:, 0:1]
    ssm_v[...] = (pre_v[...] * scale_col * gain_ref[...]).astype(BF16)
    ssm_out = pltpu.make_async_copy(ssm_v, ssm_hbm, loc.at[12])
    ssm_out.start()

    def attend_row(d):
        core_copy(d).wait_recv()
        attend(
            kvbuf[0, z - d].reshape(2 * TOK, HEAD_DIM), kvbuf[1, z - d].reshape(2 * TOK, HEAD_DIM),
            None, False,
        )

    def to_core(d, carry):
        for p in range(3):
            x_copy(d, p).wait_recv()
        core_copy(d).start()

        @pl.when(d > 1)
        def _():
            attend_row(d - 1)

        return carry

    lax.fori_loop(1, z + 1, to_core, 0)

    @pl.when(z > 0)
    def _():
        attend_row(z)

    result = o_v[...] / l_v[...]
    for h in range(2):
        attn_v[:, h * HEAD_DIM : (h + 1) * HEAD_DIM] = result[
            :, h * TOK : (h + 1) * TOK
        ].T.astype(BF16)
    attn_out = pltpu.make_async_copy(attn_v, attn_hbm, loc.at[13])
    attn_out.start()

    @pl.when(c < N_CTX - 1)
    def _():
        for cp in halo_copies():
            cp.wait_send()

    remote(dec_in.at[three], dec_in.at[three], d_s, d_r, c, sib).wait_send()
    remote(st_send.at[three], in_a.at[three], a_s, a_r, c, sib).wait_send()
    remote(out_b.at[three], in_b.at[three], b_s, b_r, c, sib).wait_send()

    @pl.when(grp < 3)
    def _():
        e_copy().wait_send()

    def kv1_sent(d, carry):
        kv1_copy(d).wait_send()
        return carry

    lax.fori_loop(1, ROWS_Z - z, kv1_sent, 0)

    def row_sent(d, carry):
        for p in range(3):
            x_copy(d, p).wait_send()
        core_copy(d).wait_send()
        return carry

    lax.fori_loop(1, z + 1, row_sent, 0)
    for p in (1, 2):
        x_copy(0, p).wait_send()
    core_copy_own().wait_send()
    for cp in quad_copies():
        cp.wait_send()
    ssm_out.wait()
    attn_out.wait()


def hand_over(ssm_in, attn_in, ssm_ref, attn_ref, sems):
    copies = [
        pltpu.make_async_copy(ssm_in, ssm_ref, sems.at[0]),
        pltpu.make_async_copy(attn_in, attn_ref, sems.at[1]),
    ]
    for cp in copies:
        cp.start()
    for cp in copies:
        cp.wait()


def local(
    x_in, z_in, bc_in, dt_raw, a_log, d_skip, conv_x, conv_bc, norm_gain, queries, keys_values
):
    hbm = pl.BlockSpec(memory_space=pltpu.HBM)
    dma = pltpu.SemaphoreType.DMA
    out_shape = (
        jax.ShapeDtypeStruct((TOK, CHAN), BF16),
        jax.ShapeDtypeStruct((TOK, 2 * HEAD_DIM), BF16),
    )
    mixed = pl.pallas_call(
        kernel,
        out_shape=out_shape,
        in_specs=[hbm] * 11,
        out_specs=(hbm, hbm),
        scratch_shapes=[
            pltpu.VMEM((HEADS, TOK), F32),
            pltpu.SMEM((HEADS,), F32),
            pltpu.SMEM((HEADS,), F32),
            pltpu.VMEM((CONV, CHAN), BF16),
            pltpu.VMEM((CONV, 2 * GROUPS * STATE), BF16),
            pltpu.VMEM((1, CHAN), F32),
            pltpu.VMEM((TOK, CHAN), BF16),
            pltpu.VMEM((TOK, CHAN), BF16),
            pltpu.VMEM((TOK, STATE), BF16),
            pltpu.VMEM((TOK, STATE), BF16),
            pltpu.VMEM((TOK, 2 * HEAD_DIM), BF16),
            pltpu.VMEM((2 * TOK, HEAD_DIM), BF16),
            pltpu.VMEM((2, ROWS_Z, 2, 2, 2, QUART, HEAD_DIM), BF16),
            pltpu.VMEM((16, CHAN), BF16),
            pltpu.VMEM((2, 16, STATE), BF16),
            pltpu.VMEM((8 + TOK, CHAN), F32),
            pltpu.VMEM((8 + TOK, 2 * STATE), F32),
            pltpu.VMEM((TOK, STATE), F32),
            pltpu.VMEM((4, SLICE, CHAN), BF16),
            pltpu.VMEM((4, SLICE, CHAN), BF16),
            pltpu.VMEM((4, SLICE, CHAN), BF16),
            pltpu.VMEM((4, SLICE, CHAN), BF16),
            pltpu.VMEM((SLICE, CHAN), BF16),
            pltpu.VMEM((SLICE, CHAN), BF16),
            pltpu.VMEM((1, CHAN), F32),
            pltpu.VMEM((4, 1, CHAN), F32),
            pltpu.VMEM((TOK, CHAN), F32),
            pltpu.VMEM((TOK, CHAN), F32),
            pltpu.VMEM((TOK, CHAN), F32),
            pltpu.VMEM((TOK, STATE), BF16),
            pltpu.VMEM((4, 1, TOK), F32),
            pltpu.VMEM((1, 2 * TOK), F32),
            pltpu.VMEM((1, 2 * TOK), F32),
            pltpu.VMEM((HEAD_DIM, 2 * TOK), F32),
            pltpu.VMEM((TOK, CHAN), BF16),
            pltpu.VMEM((TOK, 2 * HEAD_DIM), BF16),
            dma((14,)), dma((3,)), dma((3,)),
            dma(()), dma(()), dma(()), dma(()), dma(()), dma(()), dma(()), dma(()),
            dma((3,)), dma((3,)), dma((ROWS_Z,)), dma((ROWS_Z,)),
            dma((ROWS_Z, 3)), dma((ROWS_Z, 3)), dma((ROWS_Z,)), dma((ROWS_Z,)),
            pltpu.SemaphoreType.REGULAR((3,)),
        ],
        compiler_params=pltpu.CompilerParams(
            collective_id=0, has_side_effects=True, vmem_limit_bytes=64 * 1024 * 1024
        ),
        name="mixer",
    )(
        x_in, z_in, bc_in, dt_raw, a_log, d_skip, conv_x, conv_bc,
        norm_gain.reshape(1, CHAN), queries,
        keys_values.reshape(2, 2, 2, QUART, GROUPS * HEAD_DIM),
    )
    return pl.pallas_call(
        hand_over,
        out_shape=out_shape,
        in_specs=[hbm, hbm],
        out_specs=(hbm, hbm),
        scratch_shapes=[dma((2,))],
        name="hand_over",
    )(*mixed)


def solution(mesh):
    placed = (
        P("ctx", "head"),
        P("ctx", "head"),
        P("ctx", None),
        P("head", "ctx"),
        P("head"),
        P("head"),
        P(None, "head"),
        P(),
        P("head"),
        P("ctx", "head"),
        P(None, "ctx", None),
    )
    return jax.shard_map(
        local,
        mesh=mesh,
        in_specs=placed,
        out_specs=(P("ctx", "head"), P("ctx", "head")),
        check_vma=False,
    )
```

time: 50.6 us -> 53 us (1.047)
  the two profiles are of different devices: /device:TPU:1 before, /device:TPU:505 now
where the time goes in v2:
time: 53 us; the launch traced here: 52.9 us
  Pallas kernels  52.2 us (98%)
  between operations  0.64 us (1%)
    pallas_call x1, Pallas kernels, local(): pl.pallas_call(kernel, out_shape=out_shape, in_specs=[hbm] * 11, out_spec...  39.2 us
    pallas_call x1, Pallas kernels, local(): pl.pallas_call(hand_over, out_shape=out_shape, in_specs=[hbm, hbm], out_s...  13 us

profile of v2, /device:TPU:505, one launch (start us, length us, event | category | flops | bytes accessed | tf_op | source)
XLA Modules:
  0.0 52.9 jit_solution(15246158742528169456)
XLA Ops:
  0.6 39.2 %mixer.1 = (bf16[256,512]{1,0:T(8,128)(2,1)}, bf16[256,256]{1,0:T(8,128)(2,1)}) custom-call(bf16[256,512]{1,0:T(8,128)(2,1)} %x_hbm.1, bf16[256,512]{1,0:T(8,128)(2,1)} %z_hbm.1, bf16[256,2048]{1,0:T(8,128)(2,1)} %bc_hbm.1, f32[8,256]{1,0:T(8,128)} %dt_hbm.1, f32[8]{0:T(128)} %alog_hbm.1, f32[8]{0:T(128)} %dskip_hbm.1, bf16[4,512]{1,0:T(4,128)(2,1)} %cx_hbm.1, ...), custom_call_target="tpu_custom_call" | custom-call | tf_op jit(solution)/shard_map/mixer/pallas_call | solution.py:491
  39.8 13.0 %hand_over.1 = (bf16[256,512]{1,0:T(8,128)(2,1)}, bf16[256,256]{1,0:T(8,128)(2,1)}) custom-call(bf16[256,512]{1,0:T(8,128)(2,1)} %get-tuple-element.4.ssm_in, bf16[256,256]{1,0:T(8,128)(2,1)} %get-tuple-element.5.attn_in), custom_call_target="tpu_custom_call" | custom-call | tf_op jit(solution)/shard_map/hand_over/pallas_call | solution.py:548

commit v3 on v2

--- a/solution.py
+++ b/solution.py
@@ -18,7 +18,7 @@
 N_CTX = 16
 BLOCK = 128
 ROWS_Z = 8
-SLICE = STATE // 4
+SLICE = STATE // 8
 QUART = TOK // 4
 EPSILON = 1e-05
 NEGATIVE = -1e30
@@ -49,13 +49,16 @@
     st_send, in_a, out_b, in_b, e_out, e_in, dec_send, dec_in, pre_v, sz_v, ecx_v, cb_v, sq_v,
     m_v, l_v, o_v, ssm_v, attn_v,
     loc, h_s, h_r, d_s, d_r, a_s, a_r, b_s, b_r, e_s, e_r, q_s, q_r, s1_s, s1_r,
-    x_s, x_r, c_s, c_r, rdy,
+    x_s, x_r, c_s, c_r, rdy, rdy_e,
 ):
     c = lax.axis_index("ctx")
     hd = lax.axis_index("head")
     z, xh = lax.div(c, 2), lax.rem(c, 2)
-    grp, mem = lax.div(c, 4), lax.rem(c, 4)
-    zodd = lax.rem(z, 2)
+    late = lax.div(c, 8)
+    grp = lax.div(c, 4) - lax.div(c, 12)
+    mem = (1 - late) * lax.rem(c, 4) + late * (c - 8)
+    z_first = 2 * grp
+    z_last = z_first + 1 + 2 * late
     y, qi = lax.div(hd, 4), lax.rem(hd, 4)
     xl, core = lax.div(qi, 2), lax.rem(qi, 2)
     flip_c = 1 - 2 * xh
@@ -63,7 +66,15 @@
     sib = hd + 1 - 2 * core
     ycol = pl.multiple_of(y * 128, 128)
     ycol2 = pl.multiple_of(GROUPS * STATE + y * 128, 128)
-    mates = [lax.rem(mem + e, 4) for e in (1, 2, 3)]
+
+    def for_group(act):
+        @pl.when(late == 0)
+        def _():
+            act(4, 2, [lax.rem(mem + e, 4) for e in range(1, 4)])
+
+        @pl.when(late == 1)
+        def _():
+            act(8, 1, [lax.rem(mem + e, 8) for e in range(1, 8)])
 
     def remote(src, dst, ss, rs, ctx, head):
         return pltpu.make_async_remote_copy(
@@ -96,8 +107,11 @@
     def greet(ctx, head):
         pl.semaphore_signal(barrier, inc=1, device_id=(ctx, head), device_id_type=MESH)
 
-    for to in mates:
-        greet(c - mem + to, hd)
+    def greet_mates(size, each, mates):
+        for to in mates:
+            greet(c - mem + to, hd)
+
+    for_group(greet_mates)
     greet(c, sib)
     greet(c, hd + flip_l)
     greet(c, sib + flip_l)
@@ -107,11 +121,16 @@
     def _():
         greet(c - 1, hd)
 
+    @pl.when(grp == 1)
+    def _():
+        for k in range(2):
+            greet(8 + 2 * mem + k, hd)
+
     def greet_later(d, carry):
         greet(c + 2 * d, hd)
         return carry
 
-    lax.fori_loop(2 - zodd, ROWS_Z - z, greet_later, 0)
+    lax.fori_loop(z_last + 1 - z, ROWS_Z - z, greet_later, 0)
 
     for cp in small:
         cp.wait()
@@ -137,26 +156,7 @@
     tail = jnp.exp(last - cum) * step
     tail_x = jnp.dot(tail.T, spread, precision=HIGH, preferred_element_type=F32)
 
-    taps_b = cbc_ref[:, pl.ds(ycol, 128)].astype(F32)
-    taps_c = cbc_ref[:, pl.ds(ycol2, 128)].astype(F32)
-    taps_x = cx_ref[...].astype(F32)
-    pad_bc[0:8] = jnp.zeros((8, 2 * STATE), F32)
-    pad_x[0:8] = jnp.zeros((8, CHAN), F32)
-    load_b.wait()
-    load_c.wait()
-    pad_bc[8:, 0:STATE] = b_v[...].astype(F32)
-    pad_bc[8:, STATE:] = c_v[...].astype(F32)
-
-    def convolve(rows):
-        bf_v[0:rows] = conv_rows(pad_bc, taps_b, pl.ds(0, STATE), rows)
-        cb_v[0:rows] = conv_rows(pad_bc, taps_c, pl.ds(STATE, STATE), rows).astype(BF16)
-        x_v[0:rows] = conv_rows(pad_x, taps_x, pl.ds(0, CHAN), rows).astype(BF16)
-
-    load_x.wait()
-    pad_x[8:] = x_v[...].astype(F32)
-    convolve(TOK)
-
-    greeted = 3 + 4 + 2 * grp + jnp.where((mem == 3) & (c < N_CTX - 1), 1, 0)
+    greeted = 3 + 4 * late + 4 + 2 * grp + late + jnp.where((mem == 3) & (late == 0), 1, 0)
     pl.semaphore_wait(barrier, greeted)
 
     def halo_copies():
@@ -181,18 +181,25 @@
     def dec_copy(to):
         return remote(dec_send, dec_in.at[mem], d_s, d_r, c - mem + to, hd)
 
-    for to in mates:
-        dec_copy(to).start()
-
-    for far in (1, 2, 3):
-
-        @pl.when(grp >= far)
-        def _():
-            for odd in range(2):
-                pl.semaphore_signal(
-                    rdy.at[far - 1], inc=1, device_id=(4 * (grp - far) + 2 * odd + xh, hd),
-                    device_id_type=MESH,
-                )
+    def dec_start(size, each, mates):
+        for to in mates:
+            dec_copy(to).start()
+
+    for_group(dec_start)
+
+    def say_ready(sem, ctx):
+        pl.semaphore_signal(sem, inc=1, device_id=(ctx, hd), device_id_type=MESH)
+
+    @pl.when(grp == 1)
+    def _():
+        for row in range(2):
+            say_ready(rdy.at[0], 2 * row + xh)
+
+    @pl.when(grp == 2)
+    def _():
+        for row in range(4):
+            say_ready(rdy.at[1], 2 * row + xh)
+        say_ready(rdy_e, 4 + lax.div(mem, 2))
 
     def kv1_copy(d):
         return remote(
@@ -204,12 +211,17 @@
         piece = kvbuf.at[:, z - d, xh, xl, core]
         return remote(piece, piece, s1_s.at[d], s1_r.at[d], c, sib)
 
-    def kv1_group(far):
-        @pl.when(grp + far < 4)
+    def kv1_start(d, carry):
+        kv1_copy(d).start()
+        return carry
+
+    def kv1_group(grps, to_grp):
+        @pl.when((grp >= grps[0]) & (grp <= grps[-1]))
         def _():
-            pl.semaphore_wait(rdy.at[far - 1], 2)
-            for odd in range(2):
-                kv1_copy(2 * far + odd - zodd).start()
+            rows = 2 * to_grp
+            pl.semaphore_wait(rdy.at[to_grp - 1], rows)
+            for row in range(rows):
+                kv1_copy(rows + row - z).start()
 
     def x_copy(d, p):
         fh, fl = PEERS[p]
@@ -223,6 +235,30 @@
     def core_copy_own():
         piece = kvbuf.at[:, z, 1 - xh, :, core]
         return remote(piece, piece, c_s.at[0], c_r.at[0], c, sib)
+
+    load_kv.wait()
+    for p in (1, 2):
+        x_copy(0, p).start()
+    lax.fori_loop(1, z_last + 1 - z, kv1_start, 0)
+
+    taps_b = cbc_ref[:, pl.ds(ycol, 128)].astype(F32)
+    taps_c = cbc_ref[:, pl.ds(ycol2, 128)].astype(F32)
+    taps_x = cx_ref[...].astype(F32)
+    pad_bc[0:8] = jnp.zeros((8, 2 * STATE), F32)
+    pad_x[0:8] = jnp.zeros((8, CHAN), F32)
+    load_b.wait()
+    load_c.wait()
+    pad_bc[8:, 0:STATE] = b_v[...].astype(F32)
+    pad_bc[8:, STATE:] = c_v[...].astype(F32)
+
+    def convolve(rows):
+        bf_v[0:rows] = conv_rows(pad_bc, taps_b, pl.ds(0, STATE), rows)
+        cb_v[0:rows] = conv_rows(pad_bc, taps_c, pl.ds(STATE, STATE), rows).astype(BF16)
+        x_v[0:rows] = conv_rows(pad_x, taps_x, pl.ds(0, CHAN), rows).astype(BF16)
+
+    load_x.wait()
+    pad_x[8:] = x_v[...].astype(F32)
+    convolve(TOK)
 
     @pl.when(c > 0)
     def _():
@@ -236,24 +272,22 @@
     b_t = bf_v[...].T.astype(BF16)
     carried = (tail_x * x_v[...].astype(F32)).astype(BF16)
     state = jnp.dot(b_t, carried, preferred_element_type=F32).astype(BF16)
-    st_send[...] = state.reshape(4, SLICE, CHAN)
-
-    def a_copy(to):
-        return remote(st_send.at[to], in_a.at[mem], a_s, a_r, c - mem + to, hd)
-
-    for to in mates:
-        a_copy(to).start()
-    in_a[mem] = st_send[mem]
-
-    load_kv.wait()
-    for p in (1, 2):
-        x_copy(0, p).start()
-
-    @pl.when(zodd == 0)
-    def _():
-        kv1_copy(1).start()
-
-    kv1_group(1)
+    st_send[...] = state.reshape(8, SLICE, CHAN)
+
+    def a_start(size, each, mates):
+        for to in mates:
+            remote(
+                st_send.at[pl.ds(each * to, each)], in_a.at[mem, pl.ds(0, each)],
+                a_s, a_r, c - mem + to, hd,
+            ).start()
+        in_a[mem, 0:each] = st_send[pl.ds(each * mem, each)]
+
+    def a_all(size, each):
+        some = pl.ds(0, (size - 1) * each)
+        return remote(st_send.at[some], st_send.at[some], a_s, a_r, c, sib)
+
+    for_group(a_start)
+    kv1_group((0,), 1)
 
     scores = jnp.dot(cb_v[...], b_t, preferred_element_type=F32)
     t_at = lax.broadcasted_iota(jnp.int32, (TOK, TOK), 0)
@@ -282,41 +316,7 @@
     load_z.wait()
     sz_v[...] = silu(z_v[...].astype(F32))
 
-    three = pl.ds(0, 3)
-
-    def e_copy():
-        return remote(e_out, e_in, e_s, e_r, c + 4, hd)
-
-    remote(dec_in.at[three], dec_in.at[three], d_s, d_r, c, sib).wait_recv()
-    remote(st_send.at[three], in_a.at[three], a_s, a_r, c, sib).wait_recv()
-
-    @pl.when(grp > 0)
-    def _():
-        e_copy().wait_recv()
-
-    @pl.when(grp == 0)
-    def _():
-        e_in[...] = jnp.zeros_like(e_in)
-
-    running = e_in[...].astype(F32)
-    for k in range(4):
-        out_b[k] = running.astype(BF16)
-        running = jnp.exp(dec_in[k]) * running + in_a[k].astype(F32)
-    e_out[...] = running.astype(BF16)
-
-    @pl.when(grp < 3)
-    def _():
-        e_copy().start()
-
-    def b_copy(to):
-        return remote(out_b.at[to], in_b.at[mem], b_s, b_r, c - mem + to, hd)
-
-    for to in mates:
-        b_copy(to).start()
-    in_b[mem] = out_b[mem]
-
-    kv1_group(2)
-
+    kv1_group((1,), 2)
     for p in (1, 2):
         x_copy(0, p).wait_recv()
     core_copy_own().start()
@@ -327,29 +327,65 @@
             x_copy(d, p).start()
         return carry
 
-    lax.fori_loop(1, z + 1, forward, 0)
-
-    remote(out_b.at[three], in_b.at[three], b_s, b_r, c, sib).wait_recv()
-    entering = in_b[...].reshape(STATE, CHAN)
-    squares = jnp.zeros((TOK, 128), F32)
-    for part in range(2):
-        cols = slice(part * 256, (part + 1) * 256)
-        reach = jnp.dot(cb_v[...], entering[:, cols], preferred_element_type=F32)
-        gated = (pre_v[:, cols] + ecx_v[:, cols] * reach) * sz_v[:, cols]
-        pre_v[:, cols] = gated
-        squares = squares + gated[:, :128] * gated[:, :128] + gated[:, 128:] * gated[:, 128:]
-    sq_v[0] = jnp.sum(squares.T, axis=0, keepdims=True)
-
-    def quad_copies():
+    near = z - z_first + 1
+    lax.fori_loop(1, near, forward, 0)
+
+    def dec_all(size):
+        some = pl.ds(0, size - 1)
+        return remote(dec_in.at[some], dec_in.at[some], d_s, d_r, c, sib)
+
+    def e_copies(number):
+        if number == 0:
+            return [remote(e_out, e_in, e_s, e_r, c + 4, hd)]
         return [
-            remote(sq_v.at[0], sq_v.at[1], q_s.at[0], q_r.at[0], c, sib),
-            remote(sq_v.at[0], sq_v.at[2], q_s.at[1], q_r.at[1], c, hd + flip_l),
-            remote(sq_v.at[0], sq_v.at[3], q_s.at[2], q_r.at[2], c, sib + flip_l),
+            remote(e_out.at[pl.ds(k, 1)], e_in.at[pl.ds(0, 1)], e_s, e_r, 8 + 2 * mem + k, hd)
+            for k in range(2)
         ]
 
-    for cp in quad_copies():
-        cp.start()
-    kv1_group(3)
+    def scan(size, each, mates):
+        dec_all(size).wait_recv()
+        a_all(size, each).wait_recv()
+        part = pl.ds(0, each)
+        if size == 8:
+            remote(e_in.at[part], e_in.at[part], e_s, e_r, c, sib).wait_recv()
+        else:
+
+            @pl.when(grp == 1)
+            def _():
+                remote(e_in, e_in, e_s, e_r, c, sib).wait_recv()
+
+            @pl.when(grp == 0)
+            def _():
+                e_in[...] = jnp.zeros_like(e_in)
+
+        running = e_in[0:each].astype(F32)
+        for k in range(size):
+            out_b[k, 0:each] = running.astype(BF16)
+            running = jnp.exp(dec_in[k]) * running + in_a[k, 0:each].astype(F32)
+        if size == 4:
+            e_out[...] = running.astype(BF16)
+
+            @pl.when(grp == 0)
+            def _():
+                for cp in e_copies(0):
+                    cp.start()
+
+            @pl.when(grp == 1)
+            def _():
+                pl.semaphore_wait(rdy_e, 2)
+                for cp in e_copies(1):
+                    cp.start()
+
+        for to in mates:
+            remote(
+                out_b.at[to, part], in_b.at[pl.ds(each * mem, each)],
+                b_s, b_r, c - mem + to, hd,
+            ).start()
+        in_b[pl.ds(each * mem, each)] = out_b[mem, 0:each]
+
+    for_group(scan)
+    kv1_group((0,), 2)
+    lax.fori_loop(near, z + 1, forward, 0)
 
     def attend(keys, values, mask, first):
         logits = lax.dot_general(
@@ -392,6 +428,71 @@
             None, False,
         )
 
+    def to_core(d, carry):
+        for p in range(3):
+            x_copy(d, p).wait_recv()
+        core_copy(d).start()
+        return carry
+
+    lax.fori_loop(1, near, to_core, 0)
+
+    def b_all(size, each):
+        some = pl.ds(0, (size - 1) * each)
+        return remote(in_b.at[some], in_b.at[some], b_s, b_r, c, sib)
+
+    for_group(lambda size, each, mates: b_all(size, each).wait_recv())
+    entering = in_b[...].reshape(STATE, CHAN)
+    squares = jnp.zeros((TOK, 128), F32)
+    for part in range(2):
+        cols = slice(part * 256, (part + 1) * 256)
+        reach = jnp.dot(cb_v[...], entering[:, cols], preferred_element_type=F32)
+        gated = (pre_v[:, cols] + ecx_v[:, cols] * reach) * sz_v[:, cols]
+        pre_v[:, cols] = gated
+        squares = squares + gated[:, :128] * gated[:, :128] + gated[:, 128:] * gated[:, 128:]
+    sq_v[0] = jnp.sum(squares.T, axis=0, keepdims=True)
+
+    def quad_copies():
+        return [
+            remote(sq_v.at[0], sq_v.at[1], q_s.at[0], q_r.at[0], c, sib),
+            remote(sq_v.at[0], sq_v.at[2], q_s.at[1], q_r.at[1], c, hd + flip_l),
+            remote(sq_v.at[0], sq_v.at[3], q_s.at[2], q_r.at[2], c, sib + flip_l),
+        ]
+
+    for cp in quad_copies():
+        cp.start()
+
+    def attend_row(d):
+        core_copy(d).wait_recv()
+        attend(
+            kvbuf[0, z - d].reshape(2 * TOK, HEAD_DIM), kvbuf[1, z - d].reshape(2 * TOK, HEAD_DIM),
+            None, False,
+        )
+
+    def one_row(d, carry):
+        @pl.when(d >= near)
+        def _():
+            to_core(d, 0)
+
+        @pl.when(d > 1)
+        def _():
+            attend_row(d - 1)
+
+        return carry
+
+    lax.fori_loop(1, z + 1, one_row, 0)
+
+    @pl.when(z > 0)
+    def _():
+        attend_row(z)
+
+    result = o_v[...] / l_v[...]
+    for h in range(2):
+        attn_v[:, h * HEAD_DIM : (h + 1) * HEAD_DIM] = result[
+            :, h * TOK : (h + 1) * TOK
+        ].T.astype(BF16)
+    attn_out = pltpu.make_async_copy(attn_v, attn_hbm, loc.at[13])
+    attn_out.start()
+
     for cp in quad_copies():
         cp.wait_recv()
     group_total = sq_v[0] + sq_v[1] + sq_v[2] + sq_v[3]
@@ -401,50 +502,21 @@
     ssm_out = pltpu.make_async_copy(ssm_v, ssm_hbm, loc.at[12])
     ssm_out.start()
 
-    def attend_row(d):
-        core_copy(d).wait_recv()
-        attend(
-            kvbuf[0, z - d].reshape(2 * TOK, HEAD_DIM), kvbuf[1, z - d].reshape(2 * TOK, HEAD_DIM),
-            None, False,
-        )
-
-    def to_core(d, carry):
-        for p in range(3):
-            x_copy(d, p).wait_recv()
-        core_copy(d).start()
-
-        @pl.when(d > 1)
-        def _():
-            attend_row(d - 1)
-
-        return carry
-
-    lax.fori_loop(1, z + 1, to_core, 0)
-
-    @pl.when(z > 0)
-    def _():
-        attend_row(z)
-
-    result = o_v[...] / l_v[...]
-    for h in range(2):
-        attn_v[:, h * HEAD_DIM : (h + 1) * HEAD_DIM] = result[
-            :, h * TOK : (h + 1) * TOK
-        ].T.astype(BF16)
-    attn_out = pltpu.make_async_copy(attn_v, attn_hbm, loc.at[13])
-    attn_out.start()
-
     @pl.when(c < N_CTX - 1)
     def _():
         for cp in halo_copies():
             cp.wait_send()
 
-    remote(dec_in.at[three], dec_in.at[three], d_s, d_r, c, sib).wait_send()
-    remote(st_send.at[three], in_a.at[three], a_s, a_r, c, sib).wait_send()
-    remote(out_b.at[three], in_b.at[three], b_s, b_r, c, sib).wait_send()
-
-    @pl.when(grp < 3)
-    def _():
-        e_copy().wait_send()
+    def group_sent(size, each, mates):
+        dec_all(size).wait_send()
+        a_all(size, each).wait_send()
+        b_all(size, each).wait_send()
+
+    for_group(group_sent)
+
+    @pl.when(grp < 2)
+    def _():
+        remote(e_out, e_in, e_s, e_r, c, sib).wait_send()
 
     def kv1_sent(d, carry):
         kv1_copy(d).wait_send()
@@ -468,14 +540,21 @@
     attn_out.wait()
 
 
-def hand_over(ssm_in, attn_in, ssm_ref, attn_ref, sems):
-    copies = [
-        pltpu.make_async_copy(ssm_in, ssm_ref, sems.at[0]),
-        pltpu.make_async_copy(attn_in, attn_ref, sems.at[1]),
+def hand_over(ssm_in, attn_in, ssm_ref, attn_ref, ssm_v, attn_v, sems):
+    into = [
+        pltpu.make_async_copy(ssm_in, ssm_v, sems.at[0]),
+        pltpu.make_async_copy(attn_in, attn_v, sems.at[1]),
     ]
-    for cp in copies:
+    out = [
+        pltpu.make_async_copy(ssm_v, ssm_ref, sems.at[2]),
+        pltpu.make_async_copy(attn_v, attn_ref, sems.at[3]),
+    ]
+    for cp in into:
         cp.start()
-    for cp in copies:
+    for cp, later in zip(into, out):
+        cp.wait()
+        later.start()
+    for cp in out:
         cp.wait()
 
 
@@ -512,14 +591,14 @@
             pltpu.VMEM((8 + TOK, CHAN), F32),
             pltpu.VMEM((8 + TOK, 2 * STATE), F32),
             pltpu.VMEM((TOK, STATE), F32),
-            pltpu.VMEM((4, SLICE, CHAN), BF16),
-            pltpu.VMEM((4, SLICE, CHAN), BF16),
-            pltpu.VMEM((4, SLICE, CHAN), BF16),
-            pltpu.VMEM((4, SLICE, CHAN), BF16),
-            pltpu.VMEM((SLICE, CHAN), BF16),
-            pltpu.VMEM((SLICE, CHAN), BF16),
+            pltpu.VMEM((8, SLICE, CHAN), BF16),
+            pltpu.VMEM((8, 2, SLICE, CHAN), BF16),
+            pltpu.VMEM((8, 2, SLICE, CHAN), BF16),
+            pltpu.VMEM((8, SLICE, CHAN), BF16),
+            pltpu.VMEM((2, SLICE, CHAN), BF16),
+            pltpu.VMEM((2, SLICE, CHAN), BF16),
             pltpu.VMEM((1, CHAN), F32),
-            pltpu.VMEM((4, 1, CHAN), F32),
+            pltpu.VMEM((8, 1, CHAN), F32),
             pltpu.VMEM((TOK, CHAN), F32),
             pltpu.VMEM((TOK, CHAN), F32),
             pltpu.VMEM((TOK, CHAN), F32),
@@ -534,7 +613,8 @@
             dma(()), dma(()), dma(()), dma(()), dma(()), dma(()), dma(()), dma(()),
             dma((3,)), dma((3,)), dma((ROWS_Z,)), dma((ROWS_Z,)),
             dma((ROWS_Z, 3)), dma((ROWS_Z, 3)), dma((ROWS_Z,)), dma((ROWS_Z,)),
-            pltpu.SemaphoreType.REGULAR((3,)),
+            pltpu.SemaphoreType.REGULAR((2,)),
+            pltpu.SemaphoreType.REGULAR,
         ],
         compiler_params=pltpu.CompilerParams(
             collective_id=0, has_side_effects=True, vmem_limit_bytes=64 * 1024 * 1024
@@ -550,7 +630,9 @@
         out_shape=out_shape,
         in_specs=[hbm, hbm],
         out_specs=(hbm, hbm),
-        scratch_shapes=[dma((2,))],
+        scratch_shapes=[
+            pltpu.VMEM((TOK, CHAN), BF16), pltpu.VMEM((TOK, 2 * HEAD_DIM), BF16), dma((4,)),
+        ],
         name="hand_over",
     )(*mixed)
 

time: 53 us -> 34.8 us (0.66)
  the two profiles are of different devices: /device:TPU:505 before, /device:TPU:449 now
where the time goes in v3:
time: 34.8 us; the launch traced here: 34.7 us
  Pallas kernels  34 us (98%)
  between operations  0.64 us (2%)
    pallas_call x1, Pallas kernels, local(): pl.pallas_call(kernel, out_shape=out_shape, in_specs=[hbm] * 11, out_spec...  32.3 us
    pallas_call x1, Pallas kernels, local(): pl.pallas_call(hand_over, out_shape=out_shape, in_specs=[hbm, hbm], out_s...  1.73 us

profile of v3, /device:TPU:449, one launch (start us, length us, event | category | flops | bytes accessed | tf_op | source)
XLA Modules:
  0.0 34.7 jit_solution(4670887552659362668)
XLA Ops:
  0.6 32.3 %mixer.1 = (bf16[256,512]{1,0:T(8,128)(2,1)}, bf16[256,256]{1,0:T(8,128)(2,1)}) custom-call(bf16[256,512]{1,0:T(8,128)(2,1)} %x_hbm.1, bf16[256,512]{1,0:T(8,128)(2,1)} %z_hbm.1, bf16[256,2048]{1,0:T(8,128)(2,1)} %bc_hbm.1, f32[8,256]{1,0:T(8,128)} %dt_hbm.1, f32[8]{0:T(128)} %alog_hbm.1, f32[8]{0:T(128)} %dskip_hbm.1, bf16[4,512]{1,0:T(4,128)(2,1)} %cx_hbm.1, ...), custom_call_target="tpu_custom_call" | custom-call | tf_op jit(solution)/shard_map/mixer/pallas_call | solution.py:570
  33.0 1.7 %hand_over.1 = (bf16[256,512]{1,0:T(8,128)(2,1)}, bf16[256,256]{1,0:T(8,128)(2,1)}) custom-call(bf16[256,512]{1,0:T(8,128)(2,1)} %get-tuple-element.4.ssm_in, bf16[256,256]{1,0:T(8,128)(2,1)} %get-tuple-element.5.attn_in), custom_call_target="tpu_custom_call" | custom-call | tf_op jit(solution)/shard_map/hand_over/pallas_call | solution.py:628

commit v4 on v3

--- a/solution.py
+++ b/solution.py
@@ -46,10 +46,10 @@
     ssm_hbm, attn_hbm,
     dt_ref, alog_ref, dskip_ref, cx_ref, cbc_ref, gain_ref,
     x_v, z_v, b_v, c_v, q_v, q2_v, kvbuf, halo_x, halo_bc, pad_x, pad_bc, bf_v,
-    st_send, in_a, out_b, in_b, e_out, e_in, dec_send, dec_in, pre_v, sz_v, ecx_v, cb_v, sq_v,
+    st_send, in_a, out_b, in_b, e_out, e_in, t_in, lt_out, lt_in, dec_send, dec_in, pre_v, sz_v, ecx_v, cb_v, sq_v,
     m_v, l_v, o_v, ssm_v, attn_v,
-    loc, h_s, h_r, d_s, d_r, a_s, a_r, b_s, b_r, e_s, e_r, q_s, q_r, s1_s, s1_r,
-    x_s, x_r, c_s, c_r, rdy, rdy_e,
+    loc, h_s, h_r, d_s, d_r, a_s, a_r, b_s, b_r, e_s, e_r, f_s, f_r, t_s, t_r, lt_s, lt_r, q_s, q_r, s1_s, s1_r,
+    x_s, x_r, c_s, c_r, rdy, rdy_e, r_s,
 ):
     c = lax.axis_index("ctx")
     hd = lax.axis_index("head")
@@ -121,16 +121,19 @@
     def _():
         greet(c - 1, hd)
 
-    @pl.when(grp == 1)
+    @pl.when(grp < 2)
     def _():
         for k in range(2):
             greet(8 + 2 * mem + k, hd)
 
-    def greet_later(d, carry):
-        greet(c + 2 * d, hd)
-        return carry
-
-    lax.fori_loop(z_last + 1 - z, ROWS_Z - z, greet_later, 0)
+    @pl.when(grp == 0)
+    def _():
+        for row in (2, 3):
+            greet(2 * row + xh, hd)
+
+    @pl.when(grp < 2)
+    def _():
+        greet(c + 8, hd)
 
     for cp in small:
         cp.wait()
@@ -156,7 +159,7 @@
     tail = jnp.exp(last - cum) * step
     tail_x = jnp.dot(tail.T, spread, precision=HIGH, preferred_element_type=F32)
 
-    greeted = 3 + 4 * late + 4 + 2 * grp + late + jnp.where((mem == 3) & (late == 0), 1, 0)
+    greeted = 3 + 4 * late + 4 + jnp.where(grp == 1, 2, 0) + 3 * late + jnp.where((mem == 3) & (late == 0), 1, 0)
     pl.semaphore_wait(barrier, greeted)
 
     def halo_copies():
@@ -178,6 +181,20 @@
         for cp in halo_copies():
             cp.start()
 
+    def say_ready(sem, ctx):
+        pl.semaphore_signal(sem, inc=1, device_id=(ctx, hd), device_id_type=MESH)
+
+    @pl.when(grp == 1)
+    def _():
+        for row in range(2):
+            say_ready(rdy.at[0], 2 * row + xh)
+
+    @pl.when(grp == 2)
+    def _():
+        say_ready(rdy.at[1], c - 8)
+        say_ready(rdy_e, lax.div(mem, 2))
+        say_ready(rdy_e, 4 + lax.div(mem, 2))
+
     def dec_copy(to):
         return remote(dec_send, dec_in.at[mem], d_s, d_r, c - mem + to, hd)
 
@@ -186,20 +203,6 @@
             dec_copy(to).start()
 
     for_group(dec_start)
-
-    def say_ready(sem, ctx):
-        pl.semaphore_signal(sem, inc=1, device_id=(ctx, hd), device_id_type=MESH)
-
-    @pl.when(grp == 1)
-    def _():
-        for row in range(2):
-            say_ready(rdy.at[0], 2 * row + xh)
-
-    @pl.when(grp == 2)
-    def _():
-        for row in range(4):
-            say_ready(rdy.at[1], 2 * row + xh)
-        say_ready(rdy_e, 4 + lax.div(mem, 2))
 
     def kv1_copy(d):
         return remote(
@@ -215,13 +218,19 @@
         kv1_copy(d).start()
         return carry
 
-    def kv1_group(grps, to_grp):
-        @pl.when((grp >= grps[0]) & (grp <= grps[-1]))
-        def _():
-            rows = 2 * to_grp
-            pl.semaphore_wait(rdy.at[to_grp - 1], rows)
-            for row in range(rows):
-                kv1_copy(rows + row - z).start()
+    def kv1_next():
+        pl.semaphore_wait(rdy.at[0], 2)
+        for row in (2, 3):
+            kv1_copy(row - z).start()
+
+    def kv1_late():
+        pl.semaphore_wait(rdy.at[1], 1)
+        kv1_copy(4).start()
+
+    def relay_copy(e):
+        row = 4 + lax.rem(z - 4 + e, 4)
+        piece = kvbuf.at[:, z - 4, xh, xl, core]
+        return remote(piece, piece, r_s.at[e], s1_r.at[row + 4 - z], 2 * row + xh, hd)
 
     def x_copy(d, p):
         fh, fl = PEERS[p]
@@ -260,6 +269,38 @@
     pad_x[8:] = x_v[...].astype(F32)
     convolve(TOK)
 
+    def attend(keys, values, mask, first):
+        logits = lax.dot_general(
+            keys, q2_v[...], (((1,), (1,)), ((), ())), preferred_element_type=F32
+        )
+        if mask is not None:
+            logits = jnp.where(mask, logits, NEGATIVE)
+        top = jnp.max(logits, axis=0, keepdims=True)
+        if not first:
+            top = jnp.maximum(m_v[...], top)
+        grown = jnp.exp2((logits - top) * EXP_SCALE)
+        if mask is not None:
+            grown = jnp.where(mask, grown, 0.0)
+        den = jnp.sum(grown, axis=0, keepdims=True)
+        got = jnp.dot(values.T, grown.astype(BF16), preferred_element_type=F32)
+        if first:
+            l_v[...] = den
+            o_v[...] = got
+        else:
+            shrink = jnp.exp2((m_v[...] - top) * EXP_SCALE)
+            l_v[...] = l_v[...] * shrink + den
+            o_v[...] = o_v[...] * shrink + got
+        m_v[...] = top
+
+    load_q.wait()
+    q2_v[0:TOK] = q_v[:, :HEAD_DIM]
+    q2_v[TOK:] = q_v[:, HEAD_DIM:]
+    key_at = lax.broadcasted_iota(jnp.int32, (TOK, 2 * TOK), 0)
+    query_at = lax.rem(lax.broadcasted_iota(jnp.int32, (TOK, 2 * TOK), 1), TOK)
+    attend(
+        kvbuf[0, z, xh].reshape(TOK, HEAD_DIM), kvbuf[1, z, xh].reshape(TOK, HEAD_DIM),
+        key_at <= query_at, True,
+    )
     @pl.when(c > 0)
     def _():
         for cp in halo_copies():
@@ -287,7 +328,11 @@
         return remote(st_send.at[some], st_send.at[some], a_s, a_r, c, sib)
 
     for_group(a_start)
-    kv1_group((0,), 1)
+
+    @pl.when(grp == 0)
+    def _():
+        kv1_next()
+
 
     scores = jnp.dot(cb_v[...], b_t, preferred_element_type=F32)
     t_at = lax.broadcasted_iota(jnp.int32, (TOK, TOK), 0)
@@ -316,7 +361,10 @@
     load_z.wait()
     sz_v[...] = silu(z_v[...].astype(F32))
 
-    kv1_group((1,), 2)
+    @pl.when(grp == 1)
+    def _():
+        kv1_late()
+
     for p in (1, 2):
         x_copy(0, p).wait_recv()
     core_copy_own().start()
@@ -330,51 +378,61 @@
     near = z - z_first + 1
     lax.fori_loop(1, near, forward, 0)
 
+    @pl.when(late == 1)
+    def _():
+        kv1_got(4).wait_recv()
+        for e in range(1, 4):
+            relay_copy(e).start()
+        for p in range(3):
+            x_copy(4, p).start()
+
     def dec_all(size):
         some = pl.ds(0, size - 1)
         return remote(dec_in.at[some], dec_in.at[some], d_s, d_r, c, sib)
 
-    def e_copies(number):
-        if number == 0:
-            return [remote(e_out, e_in, e_s, e_r, c + 4, hd)]
-        return [
-            remote(e_out.at[pl.ds(k, 1)], e_in.at[pl.ds(0, 1)], e_s, e_r, 8 + 2 * mem + k, hd)
-            for k in range(2)
-        ]
+    one = pl.ds(0, 1)
+
+    def e_copy():
+        return remote(e_out, e_in, e_s, e_r, c + 4, hd)
+
+    def to_late(src, dst, sem, got):
+        return [remote(src(k), dst, sem, got, 8 + 2 * mem + k, hd) for k in range(2)]
 
     def scan(size, each, mates):
         dec_all(size).wait_recv()
         a_all(size, each).wait_recv()
         part = pl.ds(0, each)
+
+        def steps(state, keep):
+            for k in range(size):
+                if keep:
+                    out_b[k, 0:each] = state.astype(BF16)
+                state = jnp.exp(dec_in[k]) * state + in_a[k, 0:each].astype(F32)
+            return state
+
         if size == 8:
-            remote(e_in.at[part], e_in.at[part], e_s, e_r, c, sib).wait_recv()
+            remote(e_in.at[one], e_in.at[one], f_s, f_r, c, sib).wait_recv()
+            remote(t_in, t_in, t_s, t_r, c, sib).wait_recv()
+            remote(lt_in, lt_in, lt_s, lt_r, c, sib).wait_recv()
+            start = jnp.exp(lt_in[...]) * e_in[0:1].astype(F32) + t_in[...].astype(F32)
+            steps(start, True)
         else:
+            e_out[...] = steps(jnp.zeros((each, SLICE, CHAN), F32), True).astype(BF16)
+
+            @pl.when(grp == 0)
+            def _():
+                e_copy().start()
 
             @pl.when(grp == 1)
             def _():
+                lt_out[...] = dec_in[0] + dec_in[1] + dec_in[2] + dec_in[3]
+                pl.semaphore_wait(rdy_e, 2)
+                for cp in to_late(lambda k: e_out.at[pl.ds(k, 1)], t_in, t_s, t_r):
+                    cp.start()
+                for cp in to_late(lambda k: lt_out, lt_in, lt_s, lt_r):
+                    cp.start()
                 remote(e_in, e_in, e_s, e_r, c, sib).wait_recv()
-
-            @pl.when(grp == 0)
-            def _():
-                e_in[...] = jnp.zeros_like(e_in)
-
-        running = e_in[0:each].astype(F32)
-        for k in range(size):
-            out_b[k, 0:each] = running.astype(BF16)
-            running = jnp.exp(dec_in[k]) * running + in_a[k, 0:each].astype(F32)
-        if size == 4:
-            e_out[...] = running.astype(BF16)
-
-            @pl.when(grp == 0)
-            def _():
-                for cp in e_copies(0):
-                    cp.start()
-
-            @pl.when(grp == 1)
-            def _():
-                pl.semaphore_wait(rdy_e, 2)
-                for cp in e_copies(1):
-                    cp.start()
+                steps(e_in[...].astype(F32), True)
 
         for to in mates:
             remote(
@@ -384,49 +442,14 @@
         in_b[pl.ds(each * mem, each)] = out_b[mem, 0:each]
 
     for_group(scan)
-    kv1_group((0,), 2)
-    lax.fori_loop(near, z + 1, forward, 0)
-
-    def attend(keys, values, mask, first):
-        logits = lax.dot_general(
-            keys, q2_v[...], (((1,), (1,)), ((), ())), preferred_element_type=F32
-        )
-        if mask is not None:
-            logits = jnp.where(mask, logits, NEGATIVE)
-        top = jnp.max(logits, axis=0, keepdims=True)
-        if not first:
-            top = jnp.maximum(m_v[...], top)
-        grown = jnp.exp2((logits - top) * EXP_SCALE)
-        if mask is not None:
-            grown = jnp.where(mask, grown, 0.0)
-        den = jnp.sum(grown, axis=0, keepdims=True)
-        got = jnp.dot(values.T, grown.astype(BF16), preferred_element_type=F32)
-        if first:
-            l_v[...] = den
-            o_v[...] = got
-        else:
-            shrink = jnp.exp2((m_v[...] - top) * EXP_SCALE)
-            l_v[...] = l_v[...] * shrink + den
-            o_v[...] = o_v[...] * shrink + got
-        m_v[...] = top
-
-    load_q.wait()
-    q2_v[0:TOK] = q_v[:, :HEAD_DIM]
-    q2_v[TOK:] = q_v[:, HEAD_DIM:]
-    key_at = lax.broadcasted_iota(jnp.int32, (TOK, 2 * TOK), 0)
-    query_at = lax.rem(lax.broadcasted_iota(jnp.int32, (TOK, 2 * TOK), 1), TOK)
-    attend(
-        kvbuf[0, z, xh].reshape(TOK, HEAD_DIM), kvbuf[1, z, xh].reshape(TOK, HEAD_DIM),
-        key_at <= query_at, True,
-    )
-    core_copy_own().wait_recv()
-
-    @pl.when(xh == 1)
-    def _():
-        attend(
-            kvbuf[0, z, 0].reshape(TOK, HEAD_DIM), kvbuf[1, z, 0].reshape(TOK, HEAD_DIM),
-            None, False,
-        )
+
+    @pl.when(grp == 0)
+    def _():
+        pl.semaphore_wait(rdy_e, 2)
+        for cp in to_late(lambda k: e_out.at[pl.ds(k, 1)], e_in.at[one], f_s, f_r):
+            cp.start()
+        kv1_late()
+
 
     def to_core(d, carry):
         for p in range(3):
@@ -434,7 +457,37 @@
         core_copy(d).start()
         return carry
 
+    def attend_row(d):
+        core_copy(d).wait_recv()
+        attend(
+            kvbuf[0, z - d].reshape(2 * TOK, HEAD_DIM), kvbuf[1, z - d].reshape(2 * TOK, HEAD_DIM),
+            None, False,
+        )
+
+    def near_row(d, carry):
+        attend_row(d)
+        return carry
+
     lax.fori_loop(1, near, to_core, 0)
+    core_copy_own().wait_recv()
+
+    @pl.when(xh == 1)
+    def _():
+        attend(
+            kvbuf[0, z, 0].reshape(TOK, HEAD_DIM), kvbuf[1, z, 0].reshape(TOK, HEAD_DIM),
+            None, False,
+        )
+
+    lax.fori_loop(1, near, near_row, 0)
+
+    def forward_far(d, carry):
+        @pl.when((late == 0) | (d < 4) | (d > 4))
+        def _():
+            forward(d, 0)
+
+        return carry
+
+    lax.fori_loop(near, z + 1, forward_far, 0)
 
     def b_all(size, each):
         some = pl.ds(0, (size - 1) * each)
@@ -461,37 +514,16 @@
     for cp in quad_copies():
         cp.start()
 
-    def attend_row(d):
-        core_copy(d).wait_recv()
-        attend(
-            kvbuf[0, z - d].reshape(2 * TOK, HEAD_DIM), kvbuf[1, z - d].reshape(2 * TOK, HEAD_DIM),
-            None, False,
-        )
-
-    def one_row(d, carry):
-        @pl.when(d >= near)
-        def _():
-            to_core(d, 0)
-
-        @pl.when(d > 1)
+    def far_row(d, carry):
+        to_core(d, 0)
+
+        @pl.when(d > near)
         def _():
             attend_row(d - 1)
 
         return carry
 
-    lax.fori_loop(1, z + 1, one_row, 0)
-
-    @pl.when(z > 0)
-    def _():
-        attend_row(z)
-
-    result = o_v[...] / l_v[...]
-    for h in range(2):
-        attn_v[:, h * HEAD_DIM : (h + 1) * HEAD_DIM] = result[
-            :, h * TOK : (h + 1) * TOK
-        ].T.astype(BF16)
-    attn_out = pltpu.make_async_copy(attn_v, attn_hbm, loc.at[13])
-    attn_out.start()
+    lax.fori_loop(near, z + 1, far_row, 0)
 
     for cp in quad_copies():
         cp.wait_recv()
@@ -502,6 +534,18 @@
     ssm_out = pltpu.make_async_copy(ssm_v, ssm_hbm, loc.at[12])
     ssm_out.start()
 
+    @pl.when(grp > 0)
+    def _():
+        attend_row(z)
+
+    result = o_v[...] / l_v[...]
+    for h in range(2):
+        attn_v[:, h * HEAD_DIM : (h + 1) * HEAD_DIM] = result[
+            :, h * TOK : (h + 1) * TOK
+        ].T.astype(BF16)
+    attn_out = pltpu.make_async_copy(attn_v, attn_hbm, loc.at[13])
+    attn_out.start()
+
     @pl.when(c < N_CTX - 1)
     def _():
         for cp in halo_copies():
@@ -514,15 +558,36 @@
 
     for_group(group_sent)
 
-    @pl.when(grp < 2)
-    def _():
-        remote(e_out, e_in, e_s, e_r, c, sib).wait_send()
+    @pl.when(grp == 0)
+    def _():
+        e_copy().wait_send()
+        remote(e_out, e_in, f_s, f_r, c, sib).wait_send()
+
+    @pl.when(grp == 1)
+    def _():
+        remote(e_out, e_in, t_s, t_r, c, sib).wait_send()
+        two = pl.ds(0, 2)
+        remote(dec_in.at[two], dec_in.at[two], lt_s, lt_r, c, sib).wait_send()
 
     def kv1_sent(d, carry):
         kv1_copy(d).wait_send()
         return carry
 
-    lax.fori_loop(1, ROWS_Z - z, kv1_sent, 0)
+    lax.fori_loop(1, z_last + 1 - z, kv1_sent, 0)
+
+    @pl.when(grp == 0)
+    def _():
+        for row in (2, 3):
+            kv1_copy(row - z).wait_send()
+
+    @pl.when(late == 0)
+    def _():
+        kv1_copy(4).wait_send()
+
+    @pl.when(late == 1)
+    def _():
+        for e in range(1, 4):
+            relay_copy(e).wait_send()
 
     def row_sent(d, carry):
         for p in range(3):
@@ -597,6 +662,9 @@
             pltpu.VMEM((8, SLICE, CHAN), BF16),
             pltpu.VMEM((2, SLICE, CHAN), BF16),
             pltpu.VMEM((2, SLICE, CHAN), BF16),
+            pltpu.VMEM((1, SLICE, CHAN), BF16),
+            pltpu.VMEM((1, CHAN), F32),
+            pltpu.VMEM((1, CHAN), F32),
             pltpu.VMEM((1, CHAN), F32),
             pltpu.VMEM((8, 1, CHAN), F32),
             pltpu.VMEM((TOK, CHAN), F32),
@@ -611,10 +679,11 @@
             pltpu.VMEM((TOK, 2 * HEAD_DIM), BF16),
             dma((14,)), dma((3,)), dma((3,)),
             dma(()), dma(()), dma(()), dma(()), dma(()), dma(()), dma(()), dma(()),
+            dma(()), dma(()), dma(()), dma(()), dma(()), dma(()),
             dma((3,)), dma((3,)), dma((ROWS_Z,)), dma((ROWS_Z,)),
             dma((ROWS_Z, 3)), dma((ROWS_Z, 3)), dma((ROWS_Z,)), dma((ROWS_Z,)),
             pltpu.SemaphoreType.REGULAR((2,)),
-            pltpu.SemaphoreType.REGULAR,
+            pltpu.SemaphoreType.REGULAR, dma((4,)),
         ],
         compiler_params=pltpu.CompilerParams(
             collective_id=0, has_side_effects=True, vmem_limit_bytes=64 * 1024 * 1024

time: 34.8 us -> 33.6 us (0.966)
  the two profiles are of different devices: /device:TPU:449 before, /device:TPU:505 now
where the time goes in v4:
time: 33.6 us; the launch traced here: 33.2 us
  Pallas kernels  32.6 us (97%)
  between operations  0.64 us (2%)
    pallas_call x1, Pallas kernels, local(): pl.pallas_call(kernel, out_shape=out_shape, in_specs=[hbm] * 11, out_spec...  30.9 us
    pallas_call x1, Pallas kernels, local(): pl.pallas_call(hand_over, out_shape=out_shape, in_specs=[hbm, hbm], out_s...  1.73 us

profile of v4, /device:TPU:505, one launch (start us, length us, event | category | flops | bytes accessed | tf_op | source)
XLA Modules:
  0.0 33.2 jit_solution(12805876479209403440)
XLA Ops:
  0.6 30.9 %mixer.1 = (bf16[256,512]{1,0:T(8,128)(2,1)}, bf16[256,256]{1,0:T(8,128)(2,1)}) custom-call(bf16[256,512]{1,0:T(8,128)(2,1)} %x_hbm.1, bf16[256,512]{1,0:T(8,128)(2,1)} %z_hbm.1, bf16[256,2048]{1,0:T(8,128)(2,1)} %bc_hbm.1, f32[8,256]{1,0:T(8,128)} %dt_hbm.1, f32[8]{0:T(128)} %alog_hbm.1, f32[8]{0:T(128)} %dskip_hbm.1, bf16[4,512]{1,0:T(4,128)(2,1)} %cx_hbm.1, ...), custom_call_target="tpu_custom_call" | custom-call | tf_op jit(solution)/shard_map/mixer/pallas_call | solution.py:635
  31.5 1.7 %hand_over.1 = (bf16[256,512]{1,0:T(8,128)(2,1)}, bf16[256,256]{1,0:T(8,128)(2,1)}) custom-call(bf16[256,512]{1,0:T(8,128)(2,1)} %get-tuple-element.4.ssm_in, bf16[256,256]{1,0:T(8,128)(2,1)} %get-tuple-element.5.attn_in), custom_call_target="tpu_custom_call" | custom-call | tf_op jit(solution)/shard_map/hand_over/pallas_call | solution.py:697

commit v5 on v4

--- a/solution.py
+++ b/solution.py
@@ -64,6 +64,7 @@
     flip_c = 1 - 2 * xh
     flip_l = 2 * (1 - 2 * xl)
     sib = hd + 1 - 2 * core
+    hf = hd + flip_l
     ycol = pl.multiple_of(y * 128, 128)
     ycol2 = pl.multiple_of(GROUPS * STATE + y * 128, 128)
 
@@ -110,6 +111,7 @@
     def greet_mates(size, each, mates):
         for to in mates:
             greet(c - mem + to, hd)
+            greet(c - mem + to, hf)
 
     for_group(greet_mates)
     greet(c, sib)
@@ -155,11 +157,10 @@
     )
     spread = jnp.where(of_head, 1.0, 0.0).astype(F32)
     dec_send[...] = jnp.sum(jnp.where(of_head, last, 0.0), axis=0, keepdims=True)
-    dec_in[mem] = dec_send[...]
     tail = jnp.exp(last - cum) * step
     tail_x = jnp.dot(tail.T, spread, precision=HIGH, preferred_element_type=F32)
 
-    greeted = 3 + 4 * late + 4 + jnp.where(grp == 1, 2, 0) + 3 * late + jnp.where((mem == 3) & (late == 0), 1, 0)
+    greeted = 2 * (3 + 4 * late) + 4 + jnp.where(grp == 1, 2, 0) + 3 * late + jnp.where((mem == 3) & (late == 0), 1, 0)
     pl.semaphore_wait(barrier, greeted)
 
     def halo_copies():
@@ -196,10 +197,10 @@
         say_ready(rdy_e, 4 + lax.div(mem, 2))
 
     def dec_copy(to):
-        return remote(dec_send, dec_in.at[mem], d_s, d_r, c - mem + to, hd)
+        return remote(dec_send, dec_in.at[mem], d_s, d_r, c - mem + to, hf)
 
     def dec_start(size, each, mates):
-        for to in mates:
+        for to in mates + [mem]:
             dec_copy(to).start()
 
     for_group(dec_start)
@@ -316,16 +317,14 @@
     st_send[...] = state.reshape(8, SLICE, CHAN)
 
     def a_start(size, each, mates):
-        for to in mates:
+        for to in mates + [mem]:
             remote(
                 st_send.at[pl.ds(each * to, each)], in_a.at[mem, pl.ds(0, each)],
-                a_s, a_r, c - mem + to, hd,
+                a_s, a_r, c - mem + to, hf,
             ).start()
-        in_a[mem, 0:each] = st_send[pl.ds(each * mem, each)]
-
-    def a_all(size, each):
-        some = pl.ds(0, (size - 1) * each)
-        return remote(st_send.at[some], st_send.at[some], a_s, a_r, c, sib)
+
+    def a_all():
+        return remote(st_send, st_send, a_s, a_r, c, sib)
 
     for_group(a_start)
 
@@ -371,7 +370,7 @@
 
     def forward(d, carry):
         kv1_got(d).wait_recv()
-        for p in range(3):
+        for p in (1, 0, 2):
             x_copy(d, p).start()
         return carry
 
@@ -387,7 +386,7 @@
             x_copy(4, p).start()
 
     def dec_all(size):
-        some = pl.ds(0, size - 1)
+        some = pl.ds(0, size)
         return remote(dec_in.at[some], dec_in.at[some], d_s, d_r, c, sib)
 
     one = pl.ds(0, 1)
@@ -400,7 +399,7 @@
 
     def scan(size, each, mates):
         dec_all(size).wait_recv()
-        a_all(size, each).wait_recv()
+        a_all().wait_recv()
         part = pl.ds(0, each)
 
         def steps(state, keep):
@@ -422,6 +421,7 @@
             @pl.when(grp == 0)
             def _():
                 e_copy().start()
+                kv1_late()
 
             @pl.when(grp == 1)
             def _():
@@ -434,12 +434,11 @@
                 remote(e_in, e_in, e_s, e_r, c, sib).wait_recv()
                 steps(e_in[...].astype(F32), True)
 
-        for to in mates:
+        for to in mates + [mem]:
             remote(
                 out_b.at[to, part], in_b.at[pl.ds(each * mem, each)],
-                b_s, b_r, c - mem + to, hd,
+                b_s, b_r, c - mem + to, hf,
             ).start()
-        in_b[pl.ds(each * mem, each)] = out_b[mem, 0:each]
 
     for_group(scan)
 
@@ -448,7 +447,6 @@
         pl.semaphore_wait(rdy_e, 2)
         for cp in to_late(lambda k: e_out.at[pl.ds(k, 1)], e_in.at[one], f_s, f_r):
             cp.start()
-        kv1_late()
 
 
     def to_core(d, carry):
@@ -468,6 +466,14 @@
         attend_row(d)
         return carry
 
+    def forward_far(d, carry):
+        @pl.when((late == 0) | (d < 4) | (d > 4))
+        def _():
+            forward(d, 0)
+
+        return carry
+
+    lax.fori_loop(near, z + 1, forward_far, 0)
     lax.fori_loop(1, near, to_core, 0)
     core_copy_own().wait_recv()
 
@@ -480,20 +486,11 @@
 
     lax.fori_loop(1, near, near_row, 0)
 
-    def forward_far(d, carry):
-        @pl.when((late == 0) | (d < 4) | (d > 4))
-        def _():
-            forward(d, 0)
-
-        return carry
-
-    lax.fori_loop(near, z + 1, forward_far, 0)
-
-    def b_all(size, each):
-        some = pl.ds(0, (size - 1) * each)
-        return remote(in_b.at[some], in_b.at[some], b_s, b_r, c, sib)
-
-    for_group(lambda size, each, mates: b_all(size, each).wait_recv())
+
+    def b_all():
+        return remote(in_b, in_b, b_s, b_r, c, sib)
+
+    b_all().wait_recv()
     entering = in_b[...].reshape(STATE, CHAN)
     squares = jnp.zeros((TOK, 128), F32)
     for part in range(2):
@@ -553,8 +550,8 @@
 
     def group_sent(size, each, mates):
         dec_all(size).wait_send()
-        a_all(size, each).wait_send()
-        b_all(size, each).wait_send()
+        a_all().wait_send()
+        b_all().wait_send()
 
     for_group(group_sent)
 

time: 33.6 us -> 32.2 us (0.958)
  Pallas kernels: 32.6 us -> 31.4 us
    pallas_call x1, Pallas kernels: 30.9 us -> 29.7 us  [local(): pl.pallas_call(kernel, out_shape=out_shape, in_specs=[hbm] * 11, out_spec...]
where the time goes in v5:
time: 32.2 us; the launch traced here: 32.1 us
  Pallas kernels  31.4 us (98%)
  between operations  0.64 us (2%)
    pallas_call x1, Pallas kernels, local(): pl.pallas_call(kernel, out_shape=out_shape, in_specs=[hbm] * 11, out_spec...  29.7 us
    pallas_call x1, Pallas kernels, local(): pl.pallas_call(hand_over, out_shape=out_shape, in_specs=[hbm, hbm], out_s...  1.73 us

profile of v5, /device:TPU:505, one launch (start us, length us, event | category | flops | bytes accessed | tf_op | source)
XLA Modules:
  0.0 32.1 jit_solution(13758606470814158906)
XLA Ops:
  0.6 29.7 %mixer.1 = (bf16[256,512]{1,0:T(8,128)(2,1)}, bf16[256,256]{1,0:T(8,128)(2,1)}) custom-call(bf16[256,512]{1,0:T(8,128)(2,1)} %x_hbm.1, bf16[256,512]{1,0:T(8,128)(2,1)} %z_hbm.1, bf16[256,2048]{1,0:T(8,128)(2,1)} %bc_hbm.1, f32[8,256]{1,0:T(8,128)} %dt_hbm.1, f32[8]{0:T(128)} %alog_hbm.1, f32[8]{0:T(128)} %dskip_hbm.1, bf16[4,512]{1,0:T(4,128)(2,1)} %cx_hbm.1, ...), custom_call_target="tpu_custom_call" | custom-call | tf_op jit(solution)/shard_map/mixer/pallas_call | solution.py:632
  30.3 1.7 %hand_over.1 = (bf16[256,512]{1,0:T(8,128)(2,1)}, bf16[256,256]{1,0:T(8,128)(2,1)}) custom-call(bf16[256,512]{1,0:T(8,128)(2,1)} %get-tuple-element.4.ssm_in, bf16[256,256]{1,0:T(8,128)(2,1)} %get-tuple-element.5.attn_in), custom_call_target="tpu_custom_call" | custom-call | tf_op jit(solution)/shard_map/hand_over/pallas_call | solution.py:694

commit v6 on v5

--- a/solution.py
+++ b/solution.py
@@ -302,6 +302,10 @@
         kvbuf[0, z, xh].reshape(TOK, HEAD_DIM), kvbuf[1, z, xh].reshape(TOK, HEAD_DIM),
         key_at <= query_at, True,
     )
+    ecx_v[...] = jnp.dot(jnp.exp(cum).T, spread, precision=HIGH, preferred_element_type=F32)
+    load_z.wait()
+    sz_v[...] = silu(z_v[...].astype(F32))
+
     @pl.when(c > 0)
     def _():
         for cp in halo_copies():
@@ -356,9 +360,6 @@
                 jnp.where(left, both[0], both[1])
                 + skip_row[:, cols] * x_v[rows, cols].astype(F32)
             )
-    ecx_v[...] = jnp.dot(jnp.exp(cum).T, spread, precision=HIGH, preferred_element_type=F32)
-    load_z.wait()
-    sz_v[...] = silu(z_v[...].astype(F32))
 
     @pl.when(grp == 1)
     def _():
@@ -535,13 +536,16 @@
     def _():
         attend_row(z)
 
-    result = o_v[...] / l_v[...]
+    attn_out = []
     for h in range(2):
-        attn_v[:, h * HEAD_DIM : (h + 1) * HEAD_DIM] = result[
-            :, h * TOK : (h + 1) * TOK
-        ].T.astype(BF16)
-    attn_out = pltpu.make_async_copy(attn_v, attn_hbm, loc.at[13])
-    attn_out.start()
+        mine = slice(h * TOK, (h + 1) * TOK)
+        attn_v[h] = (o_v[:, mine] / l_v[:, mine]).T.astype(BF16)
+        attn_out.append(
+            pltpu.make_async_copy(
+                attn_v.at[h], attn_hbm.at[:, pl.ds(h * HEAD_DIM, HEAD_DIM)], loc.at[13 + h]
+            )
+        )
+        attn_out[h].start()
 
     @pl.when(c < N_CTX - 1)
     def _():
@@ -599,7 +603,8 @@
     for cp in quad_copies():
         cp.wait_send()
     ssm_out.wait()
-    attn_out.wait()
+    for cp in attn_out:
+        cp.wait()
 
 
 def hand_over(ssm_in, attn_in, ssm_ref, attn_ref, ssm_v, attn_v, sems):
@@ -673,8 +678,8 @@
             pltpu.VMEM((1, 2 * TOK), F32),
             pltpu.VMEM((HEAD_DIM, 2 * TOK), F32),
             pltpu.VMEM((TOK, CHAN), BF16),
-            pltpu.VMEM((TOK, 2 * HEAD_DIM), BF16),
-            dma((14,)), dma((3,)), dma((3,)),
+            pltpu.VMEM((2, TOK, HEAD_DIM), BF16),
+            dma((15,)), dma((3,)), dma((3,)),
             dma(()), dma(()), dma(()), dma(()), dma(()), dma(()), dma(()), dma(()),
             dma(()), dma(()), dma(()), dma(()), dma(()), dma(()),
             dma((3,)), dma((3,)), dma((ROWS_Z,)), dma((ROWS_Z,)),

time: 32.2 us -> 32.3 us (level)
  no operation moved by 1% of the time
where the time goes in v6:
time: 32.3 us; the launch traced here: 32.1 us
  Pallas kernels  31.5 us (98%)
  between operations  0.64 us (2%)
    pallas_call x1, Pallas kernels, local(): pl.pallas_call(kernel, out_shape=out_shape, in_specs=[hbm] * 11, out_spec...  29.7 us
    pallas_call x1, Pallas kernels, local(): pl.pallas_call(hand_over, out_shape=out_shape, in_specs=[hbm, hbm], out_s...  1.73 us

profile of v6, /device:TPU:505, one launch (start us, length us, event | category | flops | bytes accessed | tf_op | source)
XLA Modules:
  0.0 32.1 jit_solution(14669942239878391872)
XLA Ops:
  0.6 29.7 %mixer.1 = (bf16[256,512]{1,0:T(8,128)(2,1)}, bf16[256,256]{1,0:T(8,128)(2,1)}) custom-call(bf16[256,512]{1,0:T(8,128)(2,1)} %x_hbm.1, bf16[256,512]{1,0:T(8,128)(2,1)} %z_hbm.1, bf16[256,2048]{1,0:T(8,128)(2,1)} %bc_hbm.1, f32[8,256]{1,0:T(8,128)} %dt_hbm.1, f32[8]{0:T(128)} %alog_hbm.1, f32[8]{0:T(128)} %dskip_hbm.1, bf16[4,512]{1,0:T(4,128)(2,1)} %cx_hbm.1, ...), custom_call_target="tpu_custom_call" | custom-call | tf_op jit(solution)/shard_map/mixer/pallas_call | solution.py:637
  30.4 1.7 %hand_over.1 = (bf16[256,512]{1,0:T(8,128)(2,1)}, bf16[256,256]{1,0:T(8,128)(2,1)}) custom-call(bf16[256,512]{1,0:T(8,128)(2,1)} %get-tuple-element.4.ssm_in, bf16[256,256]{1,0:T(8,128)(2,1)} %get-tuple-element.5.attn_in), custom_call_target="tpu_custom_call" | custom-call | tf_op jit(solution)/shard_map/hand_over/pallas_call | solution.py:699

commit v7 on v5

--- a/solution.py
+++ b/solution.py
@@ -503,9 +503,9 @@
 
     def quad_copies():
         return [
+            remote(sq_v.at[0], sq_v.at[3], q_s.at[2], q_r.at[2], c, sib + flip_l),
+            remote(sq_v.at[0], sq_v.at[2], q_s.at[1], q_r.at[1], c, hd + flip_l),
             remote(sq_v.at[0], sq_v.at[1], q_s.at[0], q_r.at[0], c, sib),
-            remote(sq_v.at[0], sq_v.at[2], q_s.at[1], q_r.at[1], c, hd + flip_l),
-            remote(sq_v.at[0], sq_v.at[3], q_s.at[2], q_r.at[2], c, sib + flip_l),
         ]
 
     for cp in quad_copies():

time: 32.2 us -> 32.2 us (level)
  no operation moved by 1% of the time
where the time goes in v7:
time: 32.2 us; the launch traced here: 32.1 us
  Pallas kernels  31.4 us (98%)
  between operations  0.64 us (2%)
    pallas_call x1, Pallas kernels, local(): pl.pallas_call(kernel, out_shape=out_shape, in_specs=[hbm] * 11, out_spec...  29.7 us
    pallas_call x1, Pallas kernels, local(): pl.pallas_call(hand_over, out_shape=out_shape, in_specs=[hbm, hbm], out_s...  1.73 us

profile of v7, /device:TPU:505, one launch (start us, length us, event | category | flops | bytes accessed | tf_op | source)
XLA Modules:
  0.0 32.1 jit_solution(13022596661707512075)
XLA Ops:
  0.6 29.7 %mixer.1 = (bf16[256,512]{1,0:T(8,128)(2,1)}, bf16[256,256]{1,0:T(8,128)(2,1)}) custom-call(bf16[256,512]{1,0:T(8,128)(2,1)} %x_hbm.1, bf16[256,512]{1,0:T(8,128)(2,1)} %z_hbm.1, bf16[256,2048]{1,0:T(8,128)(2,1)} %bc_hbm.1, f32[8,256]{1,0:T(8,128)} %dt_hbm.1, f32[8]{0:T(128)} %alog_hbm.1, f32[8]{0:T(128)} %dskip_hbm.1, bf16[4,512]{1,0:T(4,128)(2,1)} %cx_hbm.1, ...), custom_call_target="tpu_custom_call" | custom-call | tf_op jit(solution)/shard_map/mixer/pallas_call | solution.py:632
  30.3 1.7 %hand_over.1 = (bf16[256,512]{1,0:T(8,128)(2,1)}, bf16[256,256]{1,0:T(8,128)(2,1)}) custom-call(bf16[256,512]{1,0:T(8,128)(2,1)} %get-tuple-element.4.ssm_in, bf16[256,256]{1,0:T(8,128)(2,1)} %get-tuple-element.5.attn_in), custom_call_target="tpu_custom_call" | custom-call | tf_op jit(solution)/shard_map/hand_over/pallas_call | solution.py:694
